TPU v7x, 32 devices: a whole 2x2x4 slice. The times are simulated.
32 devices in a mesh: dp: 4 (over y, x), tm: 8 (over z, core).
Axes of the slice: x: 2, y: 2, z: 4, core: 2. Of those that a mesh axis runs over, the one named last changes fastest.
Arguments:
- wall_inputs: bfloat16 [4, 1024, 576], P('dp', 'tm'), may hold values from -6 to 6
- in_weight: bfloat16 [576, 1024], replicated, may hold values from -0.25 to 0.25
- tap_weights: bfloat16 [1, 2048, 1024], replicated, may hold values from -0.125 to 0.125
- out_weight: bfloat16 [1024, 576], replicated, may hold values from -0.1875 to 0.1875
- cotangent: bfloat16 [4, 1024, 576], P('dp', 'tm'), may hold values from -0.09375 to 0.09375
Outputs:
- prediction: float32 [4, 1024, 576], P('dp', 'tm')
- grad_in: float32 [576, 1024], replicated
- grad_taps: float32 [1, 2048, 1024], P(None, ('dp', 'tm'))
- grad_out: float32 [1024, 576], replicated
All inputs are finite; a program needn't handle non-finite values.
Results may differ from a plain program's by a relative error of at most 0.0048.
Values may be sent and summed in bfloat16 or wider, within the bound.
A program may use at most 64 MiB of HBM per device.

v0:
```python
import jax
import jax.numpy as jnp
from jax import lax
from jax.sharding import PartitionSpec as P

LAYERS = 1
DILATION = 512


def from_behind(x, axis, by):
    size = lax.axis_size(axis)
    pairs = [(i, i + by) for i in range(size) if 0 <= i + by < size]
    return lax.ppermute(x, axis, pairs)


def project(left, weight):
    rows = left.reshape(-1, left.shape[-1])
    return jnp.dot(rows, weight, preferred_element_type=jnp.float32).reshape(
        left.shape[:-1] + (weight.shape[-1],)
    )


def project_back(left, weight):
    rows = left.reshape(-1, left.shape[-1])
    step_outcome = lax.dot_general(
        rows, weight, (((1,), (1,)), ((), ())), preferred_element_type=jnp.float32
    )
    return step_outcome.reshape(left.shape[:-1] + (weight.shape[0],))


def contract_rows(left, right):
    return lax.dot_general(
        left.reshape(-1, left.shape[-1]),
        right.reshape(-1, right.shape[-1]),
        (((0,), (0,)), ((), ())),
        preferred_element_type=jnp.float32,
    )


def lag_rows(hidden, dilation):
    shard_len = hidden.shape[1]
    whole_shards, remainder = divmod(dilation, shard_len)
    head_rows = hidden
    head_rows = from_behind(head_rows, "tm", whole_shards)
    return head_rows


def lead_sums(values, dilation):
    shard_len = values.shape[1]
    whole_shards, remainder = divmod(dilation, shard_len)
    head_rows = values
    head_rows = from_behind(head_rows.astype(jnp.bfloat16), "tm", -whole_shards).astype(
        head_rows.dtype
    )
    return head_rows


def reduce_taps(partial_value):
    per_member_split = lax.psum_scatter(partial_value, "dp", scatter_dimension=0, tiled=True)
    return lax.psum_scatter(per_member_split, "tm", scatter_dimension=0, tiled=True)


def on_device(wall_inputs, in_weight, tap_weights, out_weight, cotangent):
    channels = tap_weights.shape[2]
    hidden = project(wall_inputs, in_weight).astype(jnp.bfloat16)
    layer_at = 0
    lagged = lag_rows(hidden, DILATION)
    preact = project(lagged, tap_weights[layer_at, :channels]) + project(
        hidden, tap_weights[layer_at, channels:]
    )
    activation_function = jnp.tanh(preact)
    stored = [(lagged, hidden, activation_function)]
    hidden = (hidden.astype(jnp.float32) + activation_function).astype(jnp.bfloat16)
    prediction = project(hidden, out_weight)
    grad_out = lax.psum(contract_rows(hidden, cotangent), ("dp", "tm"))
    upstream = project_back(cotangent, out_weight)
    filter_tap_gradient = [None] * LAYERS
    for layer_at in reversed(range(LAYERS)):
        lagged, before, activation_function = stored[layer_at]
        pre_grad = (upstream * (1.0 - activation_function * activation_function)).astype(
            jnp.bfloat16
        )
        partial_value = jnp.concatenate(
            [contract_rows(lagged, pre_grad), contract_rows(before, pre_grad)], axis=0
        )
        filter_tap_gradient[layer_at] = reduce_taps(partial_value)
        direct = project_back(pre_grad, tap_weights[layer_at, channels:])
        delayed = lead_sums(project_back(pre_grad, tap_weights[layer_at, :channels]), DILATION)
        upstream = upstream + direct + delayed
    back_zero = upstream.astype(jnp.bfloat16)
    grad_in = lax.psum(contract_rows(wall_inputs, back_zero), ("dp", "tm"))
    return (prediction, grad_in, jnp.stack(filter_tap_gradient), grad_out)


def solution(mesh):
    in_specs = (P("dp", "tm", None), P(), P(), P(), P("dp", "tm", None))
    out_specs = (P("dp", "tm", None), P(), P(None, ("dp", "tm"), None), P())
    return jax.shard_map(
        on_device, mesh=mesh, in_specs=in_specs, out_specs=out_specs, check_vma=False
    )
```

profile of v0, /device:TPU:0, one launch (start us, length us, event | category | flops | bytes accessed | tf_op | source)
XLA Modules:
  0.0 240.6 jit_solution(4949643016006345441)
XLA Ops:
  8.0 0.0 reduce-scatter.3.cloned.1.call-start
  8.1 1.9 convolution_convert_fusion
  10.0 6.1 %collective-permute-start = (bf16[1,128,1024]{2,1,0:T(8,128)(2,1)S(1)}, bf16[1,128,1024]{2,1,0:T(8,128)(2,1)S(1)}, u32[]{:S(2)}, u32[]{:S(2)}) collective-permute-start(bf16[1,128,1024]{2,1,0:T(8,128)(2,1)S(1)} %bitcast.69), channel_id=1, source_target_pairs={{0,4},{1,5},{2,6},{3,7},{8,12},{9,13},{10,14},{11,15},{16,20},{17,... | collective-permute-start | bytes 786440 | tf_op jit(solution)/shard_map/ppermute | solution.py:13
  16.1 2.0 fusion.2
  18.1 3.5 %collective-permute-done = bf16[1,128,1024]{2,1,0:T(8,128)(2,1)S(1)} collective-permute-done((bf16[1,128,1024]{2,1,0:T(8,128)(2,1)S(1)}, bf16[1,128,1024]{2,1,0:T(8,128)(2,1)S(1)}, u32[]{:S(2)}, u32[]{:S(2)}) %collective-permute-start) | collective-permute-done | bytes 262176 | tf_op jit(solution)/shard_map/ppermute | solution.py:13
  21.6 0.5 fusion.15
  22.1 0.4 multiply_convert_fusion
  22.5 0.7 fusion.45
  23.3 0.7 fusion.36
  24.0 4.1 %pad_maximum_fusion = f32[2048,1024]{1,0:T(8,128)} fusion(f32[1024,1024]{1,0:T(8,128)S(1)} %fusion.45, f32[1024,1024]{1,0:T(8,128)S(1)} %fusion.36), kind=kLoop, calls=%fused_computation | loop fusion | flops 2097152 | bytes 16777216 | tf_op jit(solution)/shard_map/concatenate | solution.py:83
  28.1 0.0 reduce-scatter.3.cloned.1.call-update
  28.1 0.0 all-reduce.3.cloned.1.call-start
  28.1 2.4 %fusion.27 = bf16[1,128,1024]{2,1,0:T(8,128)(2,1)S(1)} fusion(bf16[128,1024]{1,0:T(8,128)(2,1)S(1)} %get-tuple-element.6, bf16[1,2048,1024]{2,1,0:T(8,128)(2,1)} %param.7), kind=kOutput, calls=%fused_computation.21 | convolution fusion | flops 268566528 | bytes 2621440 | tf_op jit(solution)/shard_map/dot_general | solution.py:25
  30.6 1.4 collective-permute-start.1
  32.0 1.9 fusion.39
  33.9 6.9 %collective-permute-done.1 = bf16[1,128,1024]{2,1,0:T(8,128)(2,1)S(1)} collective-permute-done((bf16[1,128,1024]{2,1,0:T(8,128)(2,1)S(1)}, bf16[1,128,1024]{2,1,0:T(8,128)(2,1)S(1)}, u32[]{:S(2)}, u32[]{:S(2)}) %collective-permute-start.1) | collective-permute-done | bytes 262176 | tf_op jit(solution)/shard_map/ppermute | solution.py:13
  40.8 4.3 %convolution_bitcast_fusion = f32[576,1024]{1,0:T(8,128)} fusion(bf16[1,128,1024]{2,1,0:T(8,128)(2,1)S(1)} %collective-permute-done.1, f32[128,1024]{1,0:T(8,128)S(1)} %get-tuple-element.7, bf16[128,1024]{1,0:T(8,128)(2,1)S(1)} %get-tuple-element.6, bf16[1,2048,1024]{2,1,0:T(8,128)(2,1)} %param.7, bf16[1,128,576]{1,2,0:T(8,128)(2,1)S(1)} %copy-done.4), kind=kOutput, calls=%fused_computation.13 | convolution fusion | flops 419954688 | bytes 5652480 | tf_op jit(solution)/shard_map/dot_general | solution.py:32
  45.1 0.0 all-reduce.3.cloned.1.call-update
  45.1 0.0 reduce-scatter.5.cloned.1.call-start
  45.1 89.7 %reduce-scatter.3.cloned.1.call-done = f32[512,1024]{1,0:T(8,128)} async-done(((f32[2048,1024]{1,0:T(8,128)}), f32[512,1024]{1,0:T(8,128)}) %reduce-scatter.3.cloned.1.call-update) | async-done | bytes 2097168 | tf_op jit(solution)/shard_map/reduce_scatter | solution.py:59
  134.9 1.2 convolution_bitcast_fusion.1
  136.1 92.1 %all-reduce.3.cloned.1.call-done = (f32[576,1024]{1,0:T(8,128)}, f32[1024,576]{0,1:T(8,128)}) async-done(((f32[576,1024]{1,0:T(8,128)}, f32[1024,576]{0,1:T(8,128)}), (f32[576,1024]{1,0:T(8,128)}, f32[1024,576]{0,1:T(8,128)})) %all-reduce.3.cloned.1.call-update) | async-done | bytes 4718608 | tf_op jit(solution)/shard_map/psum | solution.py:91
  228.2 3.5 %copy.11 = f32[576,1024]{1,0:T(8,128)} copy(f32[576,1024]{1,0:T(8,128)} %get-tuple-element.9) | data formatting | bytes 4718592
  231.7 1.4 copy.12
  (12 shorter events, 0.1 us)
Async XLA Ops:
  8.0 14.1 %copy-start = (bf16[1024,576]{0,1:T(8,128)(2,1)S(1)}, bf16[1024,576]{0,1:T(8,128)(2,1)}, u32[]{:S(2)}) copy-start(bf16[1024,576]{0,1:T(8,128)(2,1)} %param.8) | copy-start | bytes 3538948
  8.0 126.8 %reduce-scatter.3.cloned.1.call-start = ((), (), s32[]{:S(2)}) async-start(), calls=%async_computation.2 | async-start | bytes 10485760 | tf_op jit(solution)/shard_map/reduce_scatter | solution.py:59
  8.1 13.6 %copy-start.1 = (bf16[1,2048,1024]{2,1,0:T(8,128)(2,1)S(1)}, bf16[1,2048,1024]{2,1,0:T(8,128)(2,1)}, u32[]{:S(2)}) copy-start(bf16[1,2048,1024]{2,1,0:T(8,128)(2,1)} %param.7) | copy-start | bytes 12582916
  10.0 11.7 %collective-permute-start = (bf16[1,128,1024]{2,1,0:T(8,128)(2,1)S(1)}, bf16[1,128,1024]{2,1,0:T(8,128)(2,1)S(1)}, u32[]{:S(2)}, u32[]{:S(2)}) collective-permute-start(bf16[1,128,1024]{2,1,0:T(8,128)(2,1)S(1)} %bitcast.69), channel_id=1, source_target_pairs={{0,4},{1,5},{2,6},{3,7},{8,12},{9,13},{10,14},{11,15},{16,20},{17,... | collective-permute-start | bytes 786440 | tf_op jit(solution)/shard_map/ppermute | solution.py:13
  18.1 4.0 %copy-start.3 = (bf16[1,128,576]{1,2,0:T(8,128)(2,1)S(1)}, bf16[1,128,576]{1,2,0:T(8,128)(2,1)}, u32[]{:S(2)}) copy-start(bf16[1,128,576]{1,2,0:T(8,128)(2,1)} %param.9) | copy-start | bytes 442372
  28.1 200.1 %all-reduce.3.cloned.1.call-start = ((), (), s32[]{:S(2)}) async-start(), calls=%async_computation.4 | async-start | bytes 9437184 | tf_op jit(solution)/shard_map/psum | solution.py:91
  30.6 10.2 %copy-start.4 = (bf16[1,128,576]{1,2,0:T(8,128)(2,1)S(1)}, bf16[1,128,576]{1,2,0:T(8,128)(2,1)}, u32[]{:S(2)}) copy-start(bf16[1,128,576]{1,2,0:T(8,128)(2,1)} %param.5) | copy-start | bytes 442372
  30.6 10.2 %collective-permute-start.1 = (bf16[1,128,1024]{2,1,0:T(8,128)(2,1)S(1)}, bf16[1,128,1024]{2,1,0:T(8,128)(2,1)S(1)}, u32[]{:S(2)}, u32[]{:S(2)}) collective-permute-start(bf16[1,128,1024]{2,1,0:T(8,128)(2,1)S(1)} %fusion.27), channel_id=1, source_target_pairs={{4,0},{5,1},{6,2},{7,3},{12,8},{13,9},{14,10},{15,11},{20,16},{21,... | collective-permute-start | bytes 786440 | tf_op jit(solution)/shard_map/ppermute | solution.py:13
  45.1 183.1 %reduce-scatter.5.cloned.1.call-start = ((), (), s32[]{:S(2)}) async-start(), calls=%async_computation.3 | async-start | bytes 2359296 | tf_op jit(solution)/shard_map/reduce_scatter | solution.py:60
  228.2 3.5 %copy-start.2 = (f32[1024,576]{0,1:T(8,128)S(1)}, f32[1024,576]{0,1:T(8,128)}, u32[]{:S(2)}) copy-start(f32[1024,576]{0,1:T(8,128)} %get-tuple-element.11) | copy-start | bytes 7077892
Sparse Core Ops, SparseCore 0:
  28.2 106.5 reduce-scatter.2
  137.7 36.1 reduce-scatter.4
Sparse Core Ops, SparseCore 1:
  45.2 183.0 all-reduce.2
where the time goes:
time: 241 us
  waiting for transfers between devices  192 us (80%)
  matrix products  16 us (7%)
  between operations  15.6 us (6%)
  starting transfers between devices  7.63 us (3%)
  local copies, waits for them, and re-layouts  4.95 us (2%)
  other arithmetic  4.07 us (2%)
    psum x1, waiting for transfers between devices, on_device(): grad_in = lax.psum(contract_rows(wall_inputs, back_zero), ('dp', 'tm'))  92.1 us
    reduce_scatter x1, waiting for transfers between devices, reduce_taps(): lax.psum_scatter(partial_value, 'dp', scatter_dimension=0, tiled=True)  89.7 us
    ppermute x2, waiting for transfers between devices, from_behind(): return lax.ppermute(x, axis, pairs)  10.4 us
    dot_general x4, matrix products, contract_rows(): lax.dot_general(left.reshape(-1, left.shape[-1]), right.reshape(-1, right...  7.58 us
    ppermute x2, starting transfers between devices, from_behind(): return lax.ppermute(x, axis, pairs)  7.51 us
    dot_general x4, matrix products, project(): jnp.dot(rows, weight, preferred_element_type=jnp.float32)  5.58 us
    unnamed x12, local copies, waits for them, and re-layouts  4.95 us
  transfers between devices with their start and end apart: 5, of which 4 were waited for; matrix products, arithmetic and copies ran while one was open for 5% of the time, Pallas kernels for 0%

commit v1 on v0

--- a/solution.py
+++ b/solution.py
@@ -1,6 +1,8 @@
 import jax
 import jax.numpy as jnp
 from jax import lax
+from jax.experimental import pallas as pl
+from jax.experimental.pallas import tpu as pltpu
 from jax.sharding import PartitionSpec as P
 
 LAYERS = 1
@@ -92,9 +94,256 @@
     return (prediction, grad_in, jnp.stack(filter_tap_gradient), grad_out)
 
 
+BF16 = jnp.bfloat16
+F32 = jnp.float32
+
+
+def reduce_kernel(
+    t_ref, i_ref, o_ref, p_ref,
+    t_out, i_out, o_out, p_out,
+    t_r1, i_r1, o_r1, t_s2, i_s2, o_s2, t_r2, i_r2, o_r2,
+    t_z, i_z, o_z, t_rz, i_rz, o_rz, t_fin,
+    send_sems, recv_sems,
+):
+    me = lax.axis_index("dp")
+    tm = lax.axis_index("tm")
+    z, core = tm // 2, tm % 2
+    x_peer = me + 1 - 2 * (me % 2)
+    y_peer = me + 2 - 4 * (me // 2)
+    n1 = x_peer * (1 - core) + y_peer * core
+    n2 = y_peer * (1 - core) + x_peer * core
+    far = 3 - me
+    others = [z + 1 - 2 * (z % 2), (z + 2) % 4, 3 - z]
+    twin = z * 2 + 1 - core
+
+    to_n1 = {"dp": n1, "tm": tm}
+    to_n2 = {"dp": n2, "tm": tm}
+    to_z = [{"dp": me, "tm": other * 2 + core} for other in others]
+    to_twin = {"dp": me, "tm": twin}
+
+    barrier = pltpu.get_barrier_semaphore()
+    peers = [to_n1, to_n2, to_twin] + to_z
+    for peer in peers:
+        pl.semaphore_signal(barrier, inc=1, device_id=peer, device_id_type=pl.DeviceIdType.MESH)
+    pl.semaphore_wait(barrier, len(peers))
+
+    made = []
+
+    def send(src, dst, peer):
+        at = len(made)
+        copy = pltpu.make_async_remote_copy(
+            src_ref=src, dst_ref=dst, send_sem=send_sems.at[at], recv_sem=recv_sems.at[at],
+            device_id=peer, device_id_type=pl.DeviceIdType.MESH,
+        )
+        copy.start()
+        made.append(copy)
+        return copy
+
+    def arrived(copies):
+        for copy in copies:
+            copy.wait_recv()
+
+    def over(count, body):
+        def step(at, carry):
+            body(at)
+            return carry
+
+        lax.fori_loop(0, count, step, 0)
+
+    io1 = (i_ref, i_r1, i_s2, i_r2, i_z, i_rz)
+    oo1 = (o_ref, o_r1, o_s2, o_r2, o_z, o_rz)
+    tt1 = (t_ref, t_r1, t_s2, t_r2, t_z, t_rz)
+
+    def first_hop(pack, block, slot):
+        return send(pack[0].at[block], pack[1].at[slot], to_n1)
+
+    def second_hop(pack):
+        local, r1, s2, r2 = pack[:4]
+
+        def body(at):
+            s2[at] = (local[n2, at].astype(F32) + r1[0, at].astype(F32)).astype(BF16)
+
+        over(4, body)
+        return send(s2, r2, to_n2)
+
+    def plane_sum(pack, at):
+        local, r1, _, r2 = pack[:4]
+        return local[me, at].astype(F32) + r1[1, at].astype(F32) + r2[at].astype(F32)
+
+    def z_hop(pack):
+        out, landing = pack[4], pack[5]
+
+        def body(at):
+            out[at] = plane_sum(pack, at).astype(BF16)
+
+        over(4, body)
+        return [
+            send(out.at[other], landing.at[k], to_z[k]) for k, other in enumerate(others)
+        ]
+
+    def z_sum(pack):
+        landing = pack[5]
+        total = plane_sum(pack, z)
+        for k in range(3):
+            total = total + landing[k].astype(F32)
+        return total
+
+    i_a = first_hop(io1, far, 0)
+    o_a = first_hop(oo1, far, 0)
+    i_b = first_hop(io1, n1, 1)
+    o_b = first_hop(oo1, n1, 1)
+    t_a = first_hop(tt1, far, 0)
+    t_b = first_hop(tt1, n1, 1)
+    p_copy = send(p_ref, p_out, to_z[1])
+
+    arrived([i_a])
+    i_2 = second_hop(io1)
+    arrived([o_a])
+    o_2 = second_hop(oo1)
+    arrived([i_b, i_2])
+    i_zs = z_hop(io1)
+    arrived([o_b, o_2])
+    o_zs = z_hop(oo1)
+    arrived([t_a])
+    t_2 = second_hop(tt1)
+
+    arrived(i_zs)
+    i_out[core, me, z] = z_sum(io1).astype(BF16)
+    i_mine = i_out.at[core, me, z]
+    i_ag = [send(i_mine, i_mine, peer) for peer in to_z]
+    arrived(o_zs)
+    o_out[core, me, z] = z_sum(oo1).astype(BF16)
+    o_mine = o_out.at[core, me, z]
+    o_ag = [send(o_mine, o_mine, peer) for peer in to_z]
+
+    def forward(block, peer):
+        return [
+            send(i_out.at[core, block], i_out.at[core, block], peer),
+            send(o_out.at[core, block], o_out.at[core, block], peer),
+        ]
+
+    arrived(i_ag + o_ag)
+    hop1 = forward(me, to_n1)
+    hop2 = forward(me, to_n2)
+    twin_me = forward(me, to_twin)
+    arrived([t_b, t_2])
+    t_zs = z_hop(tt1)
+
+    arrived(hop1)
+    hop3 = forward(n1, to_n2)
+    twin_n1 = forward(n1, to_twin)
+    arrived(hop2)
+    twin_n2 = forward(n2, to_twin)
+
+    arrived(t_zs)
+    total = z_sum(tt1)
+    t_fin[0] = total[:64]
+    t_fin[1] = total[64:]
+    t_twin = send(t_fin.at[1 - core], t_out.at[core], to_twin)
+    t_out[core] = t_fin[core]
+
+    arrived(hop3)
+    twin_far = forward(far, to_twin)
+    arrived([t_twin, p_copy] + twin_me + twin_n1 + twin_n2 + twin_far)
+    for copy in made:
+        copy.wait_send()
+
+
+def reduce_all(taps, inner, outer, pred):
+    vmem = pl.BlockSpec(memory_space=pltpu.VMEM)
+    t_blk, i_blk, o_blk = taps.shape[2:], inner.shape[2:], outer.shape[2:]
+    blocks = (t_blk, i_blk, o_blk)
+    scratch = []
+    for lead in ((2, 4), (4,), (4,), (4,), (3,)):
+        scratch += [pltpu.VMEM(lead + blk, BF16) for blk in blocks]
+    scratch += [
+        pltpu.VMEM((2, t_blk[0] // 2, t_blk[1]), F32),
+        pltpu.SemaphoreType.DMA((41,)),
+        pltpu.SemaphoreType.DMA((41,)),
+    ]
+    return pl.pallas_call(
+        reduce_kernel,
+        out_shape=(
+            jax.ShapeDtypeStruct((2, t_blk[0] // 2, t_blk[1]), F32),
+            jax.ShapeDtypeStruct((2, 4, 4) + i_blk, BF16),
+            jax.ShapeDtypeStruct((2, 4, 4) + o_blk, BF16),
+            jax.ShapeDtypeStruct(pred.shape, F32),
+        ),
+        in_specs=[vmem] * 4,
+        out_specs=[vmem] * 4,
+        scratch_shapes=scratch,
+        compiler_params=pltpu.CompilerParams(
+            collective_id=0, has_side_effects=True, vmem_limit_bytes=48 * 1024 * 1024
+        ),
+    )(taps, inner, outer, pred)
+
+
+def on_small_slice(wall_inputs, in_weight, tap_weights, out_weight, cotangent):
+    channels = tap_weights.shape[2]
+    wide = channels // 2
+    rows, features = wall_inputs.shape[1:]
+    half = rows // 2
+    tm = lax.axis_index("tm")
+    shards = lax.axis_size("tm")
+    early = tm < shards // 2
+    core = tm % 2
+    delayed_w, current_w = tap_weights[0, :channels], tap_weights[0, channels:]
+
+    local = jnp.stack([wall_inputs[0], cotangent[0]])
+    keep = jnp.where(early, local[:, :half], local[:, half:])
+    give = jnp.where(early, local[:, half:], local[:, :half])
+    got = lax.ppermute(give, "tm", [(i, (i + shards // 2) % shards) for i in range(shards)])
+    low, high = jnp.where(early, keep, got), jnp.where(early, got, keep)
+    pairs = jnp.stack([low, high])
+    twin = lax.ppermute(pairs, "tm", [(i, i + 1 - 2 * (i % 2)) for i in range(shards)])
+    everything = jnp.stack([pairs, twin], axis=1)
+    inputs = everything[:, :, 0].reshape(4 * half, features)
+    cots = everything[:, :, 1].reshape(4 * half, features)
+
+    hidden = project(inputs, in_weight).astype(BF16)
+    lag = hidden[: 2 * half]
+    from_lag = project(lag, delayed_w)
+    preact = project(hidden, current_w) + jnp.concatenate([jnp.zeros_like(from_lag), from_lag])
+    squash = jnp.tanh(preact)
+    hidden_1 = (hidden.astype(F32) + squash).astype(BF16)
+    own = jnp.concatenate([hidden_1[:half], hidden_1[2 * half : 3 * half]])
+    pred = project(own, out_weight)
+    upstream = project_back(cots, out_weight)
+    pre_grad = (upstream * (1.0 - squash * squash)).astype(BF16)
+    late = pre_grad[2 * half :]
+    from_late = project_back(late, delayed_w)
+    back = upstream + project_back(pre_grad, current_w) + jnp.concatenate(
+        [from_late, jnp.zeros_like(from_late)]
+    )
+    back = back.astype(BF16)
+
+    pre_cols = lax.dynamic_slice_in_dim(pre_grad, core * wide, wide, 1)
+    back_cols = lax.dynamic_slice_in_dim(back, core * wide, wide, 1)
+    hidden_cols = lax.dynamic_slice_in_dim(hidden_1, core * wide, wide, 1)
+    taps = jnp.concatenate(
+        [contract_rows(lag, pre_cols[2 * half :]), contract_rows(hidden, pre_cols)], axis=0
+    ).astype(BF16).reshape(4, 4, channels // 8, wide)
+    inner = contract_rows(inputs, back_cols).astype(BF16)
+    inner = inner.reshape(4, features // 4, 4, wide // 4).transpose(0, 2, 1, 3)
+    outer = contract_rows(hidden_cols, cots).astype(BF16).reshape(4, 4, wide // 16, features)
+
+    pred_keep = jnp.where(early, pred[:half], pred[half:])
+    pred_give = jnp.where(early, pred[half:], pred[:half])
+    t_sum, i_sum, o_sum, pred_got = reduce_all(taps, inner, outer, pred_give)
+    prediction = jnp.concatenate(
+        [jnp.where(early, pred_keep, pred_got), jnp.where(early, pred_got, pred_keep)]
+    )[None]
+    grad_taps = t_sum.transpose(1, 0, 2).reshape(1, channels // 16, channels)
+    grad_in = i_sum.transpose(1, 3, 0, 2, 4).reshape(features, channels).astype(F32)
+    grad_out = o_sum.reshape(channels, features).astype(F32)
+    return prediction, grad_in, grad_taps, grad_out
+
+
 def solution(mesh):
     in_specs = (P("dp", "tm", None), P(), P(), P(), P("dp", "tm", None))
     out_specs = (P("dp", "tm", None), P(), P(None, ("dp", "tm"), None), P())
+    small = mesh.shape["dp"] == 4 and mesh.shape["tm"] == 8
     return jax.shard_map(
-        on_device, mesh=mesh, in_specs=in_specs, out_specs=out_specs, check_vma=False
-    )
+        on_small_slice if small else on_device,
+        mesh=mesh, in_specs=in_specs, out_specs=out_specs, check_vma=False,
+    )

time: 241 us -> 104 us (0.43)
  waiting for transfers between devices: 192 us -> 9.31 us
  Pallas kernels: 0 us -> 49.3 us
  local copies, waits for them, and re-layouts: 4.95 us -> 22 us
  between operations: 15.6 us -> 0.93 us
  matrix products: 16 us -> 11.6 us
  starting transfers between devices: 7.63 us -> 4.17 us
    psum x1 -> x0, waiting for transfers between devices: 92.1 us -> none  [on_device(): grad_in = lax.psum(contract_rows(wall_inputs, back_zero), ('dp', 'tm'))]
    reduce_scatter x2 -> x0, waiting for transfers between devices: 89.7 us -> none  [the longest x1 89.7 us: reduce_taps(): lax.psum_scatter(partial_value, 'dp', scatter_dimension=0, tiled=True)]
    pallas_call x0 -> x1, Pallas kernels: none -> 49.3 us  [reduce_all(): pl.pallas_call(reduce_kernel, out_shape=(jax.ShapeDtypeStruct((2, t_blk[0...]
    convert_element_type x0 -> x3, local copies, waits for them, and re-layouts: none -> 7.29 us  [the longest x2 5.94 us: on_small_slice(): i_sum.transpose(1, 3, 0, 2, 4).reshape(features, channels).astype(F32)]
    unnamed x12 -> x38, local copies, waits for them, and re-layouts: 4.95 us -> 10 us
    reshape x0 -> x3, local copies, waits for them, and re-layouts: none -> 4.39 us  [the longest x2 3.46 us: on_small_slice(): inner = inner.reshape(4, features // 4, 4, wide // 4).transpose(0, 2, 1, 3)]
    ppermute x2, starting transfers between devices: 7.51 us -> 4.17 us  [the longest x1 4.1 us: on_small_slice(): lax.ppermute(give, 'tm', [(i, (i + shards // 2) % shards) for i in range(...]
    convert_element_type x0 -> x2, other arithmetic: none -> 3.24 us  [the longest x1 1.78 us: on_small_slice(): grad_out = o_sum.reshape(channels, features).astype(F32)]
  transfers between devices with their start and end apart: 5 -> 2, of which waited for: 4 -> 2; matrix products, arithmetic and copies ran while one was open for 5% -> 0% of each run, Pallas kernels for 0% -> 0%
where the time goes in v1:
time: 104 us
  Pallas kernels  49.3 us (47%)
  local copies, waits for them, and re-layouts  22 us (21%)
  matrix products  11.6 us (11%)
  waiting for transfers between devices  9.31 us (9%)
  other arithmetic  6.28 us (6%)
  starting transfers between devices  4.17 us (4%)
    pallas_call x1, Pallas kernels, reduce_all(): pl.pallas_call(reduce_kernel, out_shape=(jax.ShapeDtypeStruct((2, t_blk[0...  49.3 us
    unnamed x38, local copies, waits for them, and re-layouts  10 us
    ppermute x1, waiting for transfers between devices, on_small_slice(): lax.ppermute(give, 'tm', [(i, (i + shards // 2) % shards) for i in range(...  7.71 us
    convert_element_type x2, local copies, waits for them, and re-layouts, on_small_slice(): i_sum.transpose(1, 3, 0, 2, 4).reshape(features, channels).astype(F32)  5.94 us
    dot_general x4, matrix products, contract_rows(): lax.dot_general(left.reshape(-1, left.shape[-1]), right.reshape(-1, right...  5.27 us
    ppermute x1, starting transfers between devices, on_small_slice(): lax.ppermute(give, 'tm', [(i, (i + shards // 2) % shards) for i in range(...  4.1 us
    dot_general x3, matrix products, project_back(): lax.dot_general(rows, weight, (((1,), (1,)), ((), ())), preferred_element...  3.94 us
    reshape x2, local copies, waits for them, and re-layouts, on_small_slice(): inner = inner.reshape(4, features // 4, 4, wide // 4).transpose(0, 2, 1, 3)  3.46 us
  transfers between devices with their start and end apart: 2, of which 2 were waited for; matrix products, arithmetic and copies ran while one was open for 0% of the time, Pallas kernels for 0%

profile of v1, /device:TPU:0, one launch (start us, length us, event | category | flops | bytes accessed | tf_op | source)
XLA Modules:
  0.0 103.6 jit_solution(10167586320689253988)
XLA Ops:
  0.6 1.2 %copy.24 = bf16[1,128,576]{2,1,0:T(8,128)(2,1)S(1)} copy(bf16[1,128,576]{1,2,0:T(8,128)(2,1)} %param.5) | data formatting | bytes 294912 | tf_op args[0]
  1.8 1.1 %copy.25 = bf16[1,128,576]{2,1,0:T(8,128)(2,1)S(1)} copy(bf16[1,128,576]{1,2,0:T(8,128)(2,1)} %param.9) | data formatting | bytes 294912 | tf_op args[4]
  2.9 4.1 %collective-permute-start = (bf16[2,64,576]{2,1,0:T(8,128)(2,1)S(1)}, bf16[2,64,576]{2,1,0:T(8,128)(2,1)S(1)}, u32[]{:S(2)}, u32[]{:S(2)}) collective-permute-start(bf16[2,64,576]{2,1,0:T(8,128)(2,1)S(1)} %broadcast_select_fusion), channel_id=1, source_target_pairs={{0,4},{1,5},{2,6},{3,7},{4,0},{5,1},{6,2},{7,3},{8,12},{9,13},{10,... | collective-permute-start | bytes 442376 | tf_op jit(solution)/shard_map/ppermute | solution.py:295
  7.0 7.7 %collective-permute-done = bf16[2,64,576]{2,1,0:T(8,128)(2,1)S(1)} collective-permute-done((bf16[2,64,576]{2,1,0:T(8,128)(2,1)S(1)}, bf16[2,64,576]{2,1,0:T(8,128)(2,1)S(1)}, u32[]{:S(2)}, u32[]{:S(2)}) %collective-permute-start) | collective-permute-done | bytes 147488 | tf_op jit(solution)/shard_map/ppermute | solution.py:295
  15.0 1.6 %collective-permute-done.1 = bf16[2,2,64,576]{3,2,1,0:T(8,128)(2,1)S(1)} collective-permute-done((bf16[2,2,64,576]{3,2,1,0:T(8,128)(2,1)S(1)}, bf16[2,2,64,576]{3,2,1,0:T(8,128)(2,1)S(1)}, u32[]{:S(2)}, u32[]{:S(2)}) %collective-permute-start.1) | collective-permute-done | bytes 294944 | tf_op jit(solution)/shard_map/ppermute | solution.py:298
  20.0 0.9 add_convert_fusion
  21.0 1.2 %convolution_convert_fusion.2 = bf16[512,576]{0,1:T(8,128)(2,1)} fusion(bf16[256,576]{1,0:T(8,128)(2,1)S(1)} %bitcast.53, bf16[256,1024]{1,0:T(8,128)(2,1)S(1)} %get-tuple-element.24, s32[]{:T(128)S(6)} %select_n.60), kind=kOutput, calls=%fused_computation.18 | convolution fusion | flops 151289856 | bytes 1179652 | tf_op jit(solution)/shard_map/dot_general | solution.py:34
  22.2 1.6 %fusion = f32[128,1024]{1,0:T(8,128)} fusion(bf16[1,2048,1024]{2,1,0:T(8,128)(2,1)S(1)} %copy-done.16, bf16[256,1024]{1,0:T(8,128)(2,1)S(1)} %get-tuple-element.25), kind=kOutput, calls=%fused_computation.2 | convolution fusion | flops 268435456 | bytes 2883584 | tf_op jit(solution)/shard_map/dot_general | solution.py:27
  24.3 1.7 %fusion.4 = f32[256,1024]{1,0:T(8,128)} fusion(bf16[256,1024]{1,0:T(8,128)(2,1)S(1)} %get-tuple-element.25, bf16[1,2048,1024]{2,1,0:T(8,128)(2,1)S(1)} %copy-done.16), kind=kOutput, calls=%fused_computation.6 | convolution fusion | flops 536870912 | bytes 3670016 | tf_op jit(solution)/shard_map/dot_general | solution.py:27
  26.0 1.4 %copy.31 = bf16[512,576]{1,0:T(8,128)(2,1)S(1)} copy(bf16[512,576]{0,1:T(8,128)(2,1)} %convolution_convert_fusion.2) | data formatting | bytes 1179648 | tf_op jit(solution)/shard_map/convert_element_type | solution.py:328
  28.4 2.4 %convolution_convert_fusion = bf16[1024,512]{1,0:T(8,128)(2,1)} fusion(bf16[256,1024]{1,0:T(8,128)(2,1)S(1)} %copy-done.5, bf16[256,1024]{1,0:T(8,128)(2,1)} %copy-done.14, s32[]{:T(128)S(6)} %add.31, s32[]{:T(128)S(6)} %select_n.60), kind=kOutput, calls=%fused_computation.14 | convolution fusion | flops 134742016 | bytes 1441800 | tf_op jit(solution)/shard_map/dot_general | solution.py:34
  30.9 1.2 %convolution_convert_fusion.3 = bf16[576,512]{1,0:T(8,128)(2,1)} fusion(bf16[256,576]{1,0:T(8,128)(2,1)S(1)} %bitcast.55, s32[]{:T(128)S(6)} %select_n.60, f32[128,1024]{1,0:T(8,128)S(1)} %copy-done.13, f32[256,1024]{1,0:T(8,128)S(1)} %copy-done.15, f32[256,1024]{1,0:T(8,128)S(1)} %copy-done.11), kind=kOutput, calls=%fused_computation.19 | convolution fusion | flops 151683072 | bytes 2490372 | tf_op jit(solution)/shard_map/dot_general | solution.py:34
  32.1 2.3 %reshape.26 = bf16[4,144,4,128]{3,2,1,0:T(4,128)(2,1)} reshape(bf16[576,512]{1,0:T(8,128)(2,1)} %convolution_convert_fusion.3) | data formatting | bytes 1179648 | tf_op jit(solution)/shard_map/reshape | solution.py:327
  34.4 1.1 %copy.38 = bf16[4,144,4,128]{3,1,2,0:T(8,128)(2,1)S(1)} copy(bf16[4,144,4,128]{3,2,1,0:T(4,128)(2,1)} %reshape.26) | data formatting | bytes 1179648 | tf_op jit(solution)/shard_map/reshape | solution.py:327
  35.5 2.7 %pad_maximum_fusion = bf16[2048,512]{1,0:T(8,128)(2,1)} fusion(bf16[1024,512]{1,0:T(8,128)(2,1)S(1)} %convolution_convert_fusion.1, bf16[1024,512]{1,0:T(8,128)(2,1)} %convolution_convert_fusion), kind=kLoop, calls=%fused_computation.1 | loop fusion | flops 4194304 | bytes 4194304 | tf_op jit(solution)/shard_map/concatenate | solution.py:323
  38.2 49.3 %shard_map.84 = (f32[2,64,512]{2,1,0:T(8,128)S(1)}, bf16[2,4,4,144,128]{4,3,2,1,0:T(8,128)(2,1)S(1)}, bf16[2,4,4,32,576]{4,3,2,1,0:T(8,128)(2,1)S(1)}, f32[64,576]{1,0:T(8,128)S(1)}) custom-call(bf16[4,4,128,512]{3,2,1,0:T(8,128)(2,1)} %bitcast.51, bf16[4,4,144,128]{3,2,1,0:T(8,128)(2,1)S(1)} %bitcast.49, bf16[4,4,32,576]{3,2,1,0:T(8,128)(2,1)S(1)} %bitcast.48, ...), custom_call_target="tpu_custom_call" | custom-call | tf_op jit(solution)/shard_map/pallas_call | solution.py:264
  87.5 1.0 copy-done.1
  89.3 0.9 copy.34
  90.4 0.9 reshape.28
  91.3 1.5 %convert_bitcast_fusion = f32[4,144,2,4,128]{4,1,3,0,2:T(8,128)S(1)} fusion(bf16[2,4,4,144,128]{4,3,2,1,0:T(8,128)(2,1)} %copy-done.1), kind=kLoop, calls=%fused_computation | loop fusion | flops 589824 | bytes 3538944 | tf_op jit(solution)/shard_map/convert_element_type | solution.py:337
  92.8 2.3 %copy.32 = f32[4,144,2,4,128]{4,3,2,1,0:T(4,128)} copy(f32[4,144,2,4,128]{4,1,3,0,2:T(8,128)S(1)} %convert_bitcast_fusion) | data formatting | bytes 4718592 | tf_op jit(solution)/shard_map/convert_element_type | solution.py:337
  95.1 3.6 %reshape.29 = f32[576,1024]{1,0:T(8,128)} reshape(f32[4,144,2,4,128]{4,3,2,1,0:T(4,128)} %copy.32) | data formatting | bytes 4718592 | tf_op jit(solution)/shard_map/convert_element_type | solution.py:337
  98.7 1.8 %bitcast_convert_fusion = f32[1024,576]{1,0:T(8,128)} fusion(bf16[2,4,4,32,576]{4,3,2,1,0:T(8,128)(2,1)S(1)} %get-tuple-element.11), kind=kLoop, calls=%fused_computation.20 | loop fusion | flops 589824 | bytes 3538944 | tf_op jit(solution)/shard_map/convert_element_type | solution.py:338
  100.5 3.1 %copy.35 = f32[1024,576]{0,1:T(8,128)} copy(f32[1024,576]{1,0:T(8,128)} %bitcast_convert_fusion) | data formatting | bytes 4718592
  (50 shorter events, 6.1 us)
Async XLA Ops:
  0.6 18.7 %copy-start = (bf16[1024,576]{0,1:T(8,128)(2,1)S(1)}, bf16[1024,576]{0,1:T(8,128)(2,1)}, u32[]{:S(2)}) copy-start(bf16[1024,576]{0,1:T(8,128)(2,1)} %param.8) | copy-start | bytes 3538948
  2.9 14.6 %copy-start.12 = (bf16[576,1024]{1,0:T(8,128)(2,1)S(1)}, bf16[576,1024]{1,0:T(8,128)(2,1)}, u32[]{:S(2)}) copy-start(bf16[576,1024]{1,0:T(8,128)(2,1)} %param.6) | copy-start | bytes 3538948
  2.9 11.8 %collective-permute-start = (bf16[2,64,576]{2,1,0:T(8,128)(2,1)S(1)}, bf16[2,64,576]{2,1,0:T(8,128)(2,1)S(1)}, u32[]{:S(2)}, u32[]{:S(2)}) collective-permute-start(bf16[2,64,576]{2,1,0:T(8,128)(2,1)S(1)} %broadcast_select_fusion), channel_id=1, source_target_pairs={{0,4},{1,5},{2,6},{3,7},{4,0},{5,1},{6,2},{7,3},{8,12},{9,13},{10,... | collective-permute-start | bytes 442376 | tf_op jit(solution)/shard_map/ppermute | solution.py:295
  14.9 1.7 %collective-permute-start.1 = (bf16[2,2,64,576]{3,2,1,0:T(8,128)(2,1)S(1)}, bf16[2,2,64,576]{3,2,1,0:T(8,128)(2,1)S(1)}, u32[]{:S(2)}, u32[]{:S(2)}) collective-permute-start(bf16[2,2,64,576]{3,2,1,0:T(8,128)(2,1)S(1)} %get-tuple-element.34), channel_id=1, source_target_pairs={{0,1},{1,0},{2,3},{3,2},{4,5},{5,4},{6,7},{7,6},{8,9},{9,8},{10,11... | collective-permute-start | bytes 884744 | tf_op jit(solution)/shard_map/ppermute | solution.py:298
  16.6 2.3 %copy-start.16 = (bf16[1,2048,1024]{2,1,0:T(8,128)(2,1)S(1)}, bf16[1,2048,1024]{2,1,0:T(8,128)(2,1)}, u32[]{:S(2)}) copy-start(bf16[1,2048,1024]{2,1,0:T(8,128)(2,1)} %param.7) | copy-start | bytes 12582916
  16.8 0.7 copy-start.8
  18.9 4.9 %copy-start.4 = (bf16[256,1024]{1,0:T(8,128)(2,1)}, bf16[256,1024]{1,0:T(8,128)(2,1)S(1)}, u32[]{:S(2)}) copy-start(bf16[256,1024]{1,0:T(8,128)(2,1)S(1)} %convolution_convert_fusion.4) | copy-start | bytes 1572868
  20.0 1.0 copy-start.10
  21.0 3.3 %copy-start.14 = (bf16[256,1024]{1,0:T(8,128)(2,1)}, bf16[256,1024]{1,0:T(8,128)(2,1)S(1)}, u32[]{:S(2)}) copy-start(bf16[256,1024]{1,0:T(8,128)(2,1)S(1)} %get-tuple-element.25) | copy-start | bytes 1572868
  27.4 1.0 %copy-start.5 = (bf16[256,1024]{1,0:T(8,128)(2,1)S(1)}, bf16[256,1024]{1,0:T(8,128)(2,1)}, u32[]{:S(2)}) copy-start(bf16[256,1024]{1,0:T(8,128)(2,1)} %copy-done.4) | copy-start | bytes 1572868
  27.4 3.5 %copy-start.9 = (bf16[2,2,1,64,576]{4,3,1,0,2:T(8,128)(2,1)S(1)}, bf16[2,2,1,64,576]{4,3,1,0,2:T(8,128)(2,1)}, u32[]{:S(2)}) copy-start(bf16[2,2,1,64,576]{4,3,1,0,2:T(8,128)(2,1)} %copy-done.8) | copy-start | bytes 884740
  27.4 3.5 %copy-start.11 = (f32[256,1024]{1,0:T(8,128)S(1)}, f32[256,1024]{1,0:T(8,128)}, u32[]{:S(2)}) copy-start(f32[256,1024]{1,0:T(8,128)} %copy-done.10) | copy-start | bytes 3145732
  27.4 3.5 %copy-start.13 = (f32[128,1024]{1,0:T(8,128)S(1)}, f32[128,1024]{1,0:T(8,128)}, u32[]{:S(2)}) copy-start(f32[128,1024]{1,0:T(8,128)} %fusion) | copy-start | bytes 1572868
  27.4 3.5 %copy-start.15 = (f32[256,1024]{1,0:T(8,128)S(1)}, f32[256,1024]{1,0:T(8,128)}, u32[]{:S(2)}) copy-start(f32[256,1024]{1,0:T(8,128)} %fusion.4) | copy-start | bytes 3145732
  28.0 2.9 %copy-start.6 = (f32[128,576]{1,0:T(8,128)}, f32[128,576]{1,0:T(8,128)S(1)}, u32[]{:S(2)}) copy-start(f32[128,576]{1,0:T(8,128)S(1)} %fusion.23) | copy-start | bytes 884740
  38.2 51.0 %copy-start.7 = (f32[128,576]{1,0:T(8,128)S(1)}, f32[128,576]{1,0:T(8,128)}, u32[]{:S(2)}) copy-start(f32[128,576]{1,0:T(8,128)} %copy-done.6) | copy-start | bytes 884740
  87.5 1.0 copy-start.1
  88.5 0.7 copy-start.2
  89.2 1.0 copy-start.3

commit v2 on v1

--- a/solution.py
+++ b/solution.py
@@ -153,32 +153,58 @@
     io1 = (i_ref, i_r1, i_s2, i_r2, i_z, i_rz)
     oo1 = (o_ref, o_r1, o_s2, o_r2, o_z, o_rz)
     tt1 = (t_ref, t_r1, t_s2, t_r2, t_z, t_rz)
+    tall = i_s2.shape[0]
+    lanes = i_rz.shape[2]
+
+    def rows_of(block):
+        return pl.ds(pl.multiple_of(block * tall, 16), tall)
+
+    def cols_of(at):
+        return pl.ds(pl.multiple_of(at * lanes, 128), lanes)
 
     def first_hop(pack, block, slot):
-        return send(pack[0].at[block], pack[1].at[slot], to_n1)
+        flat = len(pack[0].shape) == 2
+        src = pack[0].at[rows_of(block)] if flat else pack[0].at[block]
+        return send(src, pack[1].at[slot], to_n1)
 
     def second_hop(pack):
         local, r1, s2, r2 = pack[:4]
 
         def body(at):
-            s2[at] = (local[n2, at].astype(F32) + r1[0, at].astype(F32)).astype(BF16)
+            if len(local.shape) == 2:
+                cut = cols_of(at)
+                mine = local[rows_of(n2), cut].astype(F32)
+                s2[:, cut] = (mine + r1[0, :, cut].astype(F32)).astype(BF16)
+            else:
+                s2[at] = (local[n2, at].astype(F32) + r1[0, at].astype(F32)).astype(BF16)
 
         over(4, body)
         return send(s2, r2, to_n2)
 
     def plane_sum(pack, at):
         local, r1, _, r2 = pack[:4]
-        return local[me, at].astype(F32) + r1[1, at].astype(F32) + r2[at].astype(F32)
+        if len(local.shape) == 2:
+            cut = cols_of(at)
+            mine, first, second = local[rows_of(me), cut], r1[1, :, cut], r2[:, cut]
+        else:
+            mine, first, second = local[me, at], r1[1, at], r2[at]
+        return mine.astype(F32) + first.astype(F32) + second.astype(F32)
 
     def z_hop(pack):
         out, landing = pack[4], pack[5]
+        flat = len(out.shape) == 2
 
         def body(at):
-            out[at] = plane_sum(pack, at).astype(BF16)
+            value = plane_sum(pack, at).astype(BF16)
+            if flat:
+                out[:, cols_of(at)] = value
+            else:
+                out[at] = value
 
         over(4, body)
         return [
-            send(out.at[other], landing.at[k], to_z[k]) for k, other in enumerate(others)
+            send(out.at[:, cols_of(other)] if flat else out.at[other], landing.at[k], to_z[k])
+            for k, other in enumerate(others)
         ]
 
     def z_sum(pack):
@@ -208,19 +234,19 @@
     t_2 = second_hop(tt1)
 
     arrived(i_zs)
-    i_out[core, me, z] = z_sum(io1).astype(BF16)
-    i_mine = i_out.at[core, me, z]
+    i_mine = i_out.at[rows_of(me), cols_of(core * 4 + z)]
+    i_out[rows_of(me), cols_of(core * 4 + z)] = z_sum(io1).astype(BF16)
     i_ag = [send(i_mine, i_mine, peer) for peer in to_z]
     arrived(o_zs)
-    o_out[core, me, z] = z_sum(oo1).astype(BF16)
-    o_mine = o_out.at[core, me, z]
+    o_mine = o_out.at[rows_of(me), cols_of(core * 4 + z)]
+    o_out[rows_of(me), cols_of(core * 4 + z)] = z_sum(oo1).astype(BF16)
     o_ag = [send(o_mine, o_mine, peer) for peer in to_z]
 
     def forward(block, peer):
-        return [
-            send(i_out.at[core, block], i_out.at[core, block], peer),
-            send(o_out.at[core, block], o_out.at[core, block], peer),
-        ]
+        wide = pl.ds(pl.multiple_of(core * 4 * lanes, 128), 4 * lanes)
+        i_part = i_out.at[rows_of(block), wide]
+        o_part = o_out.at[rows_of(block), wide]
+        return [send(i_part, i_part, peer), send(o_part, o_part, peer)]
 
     arrived(i_ag + o_ag)
     hop1 = forward(me, to_n1)
@@ -251,11 +277,15 @@
 
 def reduce_all(taps, inner, outer, pred):
     vmem = pl.BlockSpec(memory_space=pltpu.VMEM)
-    t_blk, i_blk, o_blk = taps.shape[2:], inner.shape[2:], outer.shape[2:]
-    blocks = (t_blk, i_blk, o_blk)
+    t_blk = taps.shape[2:]
+    features, wide = inner.shape
+    tall, lanes = features // 4, wide // 4
     scratch = []
-    for lead in ((2, 4), (4,), (4,), (4,), (3,)):
-        scratch += [pltpu.VMEM(lead + blk, BF16) for blk in blocks]
+    for lead in ((2,), (), (), ()):
+        flat = pltpu.VMEM(lead + (tall, wide), BF16)
+        scratch += [pltpu.VMEM(lead + (4,) + t_blk, BF16), flat, flat]
+    landing = pltpu.VMEM((3, tall, lanes), BF16)
+    scratch += [pltpu.VMEM((3,) + t_blk, BF16), landing, landing]
     scratch += [
         pltpu.VMEM((2, t_blk[0] // 2, t_blk[1]), F32),
         pltpu.SemaphoreType.DMA((41,)),
@@ -265,15 +295,15 @@
         reduce_kernel,
         out_shape=(
             jax.ShapeDtypeStruct((2, t_blk[0] // 2, t_blk[1]), F32),
-            jax.ShapeDtypeStruct((2, 4, 4) + i_blk, BF16),
-            jax.ShapeDtypeStruct((2, 4, 4) + o_blk, BF16),
+            jax.ShapeDtypeStruct((features, 2 * wide), BF16),
+            jax.ShapeDtypeStruct((features, 2 * wide), BF16),
             jax.ShapeDtypeStruct(pred.shape, F32),
         ),
         in_specs=[vmem] * 4,
         out_specs=[vmem] * 4,
         scratch_shapes=scratch,
         compiler_params=pltpu.CompilerParams(
-            collective_id=0, has_side_effects=True, vmem_limit_bytes=48 * 1024 * 1024
+            collective_id=0, has_side_effects=True, vmem_limit_bytes=24 * 1024 * 1024
         ),
     )(taps, inner, outer, pred)
 
@@ -320,12 +350,11 @@
     pre_cols = lax.dynamic_slice_in_dim(pre_grad, core * wide, wide, 1)
     back_cols = lax.dynamic_slice_in_dim(back, core * wide, wide, 1)
     hidden_cols = lax.dynamic_slice_in_dim(hidden_1, core * wide, wide, 1)
-    taps = jnp.concatenate(
-        [contract_rows(lag, pre_cols[2 * half :]), contract_rows(hidden, pre_cols)], axis=0
-    ).astype(BF16).reshape(4, 4, channels // 8, wide)
+    lagged = jnp.concatenate([jnp.zeros_like(lag), lag])
+    both = jnp.concatenate([lagged, hidden], axis=1)
+    taps = contract_rows(both, pre_cols).astype(BF16).reshape(4, 4, channels // 8, wide)
     inner = contract_rows(inputs, back_cols).astype(BF16)
-    inner = inner.reshape(4, features // 4, 4, wide // 4).transpose(0, 2, 1, 3)
-    outer = contract_rows(hidden_cols, cots).astype(BF16).reshape(4, 4, wide // 16, features)
+    outer = contract_rows(cots, hidden_cols).astype(BF16)
 
     pred_keep = jnp.where(early, pred[:half], pred[half:])
     pred_give = jnp.where(early, pred[half:], pred[:half])
@@ -334,8 +363,8 @@
         [jnp.where(early, pred_keep, pred_got), jnp.where(early, pred_got, pred_keep)]
     )[None]
     grad_taps = t_sum.transpose(1, 0, 2).reshape(1, channels // 16, channels)
-    grad_in = i_sum.transpose(1, 3, 0, 2, 4).reshape(features, channels).astype(F32)
-    grad_out = o_sum.reshape(channels, features).astype(F32)
+    grad_in = i_sum.astype(F32)
+    grad_out = o_sum.astype(F32).T
     return prediction, grad_in, grad_taps, grad_out
 
 

time: 104 us -> 82.7 us (0.80)
  local copies, waits for them, and re-layouts: 22 us -> 10.4 us
  matrix products: 11.6 us -> 6.03 us
  Pallas kernels: 49.3 us -> 46.8 us
  other arithmetic: 6.28 us -> 4.46 us
    convert_element_type x3 -> x0, local copies, waits for them, and re-layouts: 7.29 us -> none  [the longest x2 5.94 us: on_small_slice(): i_sum.transpose(1, 3, 0, 2, 4).reshape(features, channels).astype(F32)]
    dot_general x4 -> x3, matrix products: 5.27 us -> 1.42 us  [contract_rows(): lax.dot_general(left.reshape(-1, left.shape[-1]), right.reshape(-1, right...]
    unnamed x38 -> x15, local copies, waits for them, and re-layouts: 10 us -> 6.44 us
    reshape x2 -> x0, local copies, waits for them, and re-layouts: 3.46 us -> none  [on_small_slice(): inner = inner.reshape(4, features // 4, 4, wide // 4).transpose(0, 2, 1, 3)]
    concatenate x1 -> x0, other arithmetic: 2.68 us -> none  [on_small_slice(): jnp.concatenate([contract_rows(lag, pre_cols[2 * half:]), contract_rows(h...]
    pallas_call x1, Pallas kernels: 49.3 us -> 46.8 us  [reduce_all(): pl.pallas_call(reduce_kernel, out_shape=(jax.ShapeDtypeStruct((2, t_blk[0...]
    dot_general x3, matrix products: 3.94 us -> 2.16 us  [project_back(): lax.dot_general(rows, weight, (((1,), (1,)), ((), ())), preferred_element...]
    transpose x0 -> x1, other arithmetic: none -> 1.69 us  [on_small_slice(): grad_out = o_sum.astype(F32).T]
where the time goes in v2:
time: 82.7 us; the launch traced here: 82.1 us
  Pallas kernels  46.8 us (57%)
  local copies, waits for them, and re-layouts  10.4 us (13%)
  waiting for transfers between devices  9.31 us (11%)
  matrix products  6.03 us (7%)
  other arithmetic  4.46 us (5%)
  starting transfers between devices  4.17 us (5%)
  between operations  0.88 us (1%)
    pallas_call x1, Pallas kernels, reduce_all(): pl.pallas_call(reduce_kernel, out_shape=(jax.ShapeDtypeStruct((2, t_blk[0...  46.8 us
    ppermute x1, waiting for transfers between devices, on_small_slice(): lax.ppermute(give, 'tm', [(i, (i + shards // 2) % shards) for i in range(...  7.71 us
    unnamed x15, local copies, waits for them, and re-layouts  6.44 us
    ppermute x1, starting transfers between devices, on_small_slice(): lax.ppermute(give, 'tm', [(i, (i + shards // 2) % shards) for i in range(...  4.1 us
    dot_general x4, matrix products, project(): jnp.dot(rows, weight, preferred_element_type=jnp.float32)  2.45 us
    dot_general x3, matrix products, project_back(): lax.dot_general(rows, weight, (((1,), (1,)), ((), ())), preferred_element...  2.16 us
    reshape x1, local copies, waits for them, and re-layouts, on_small_slice(): grad_taps = t_sum.transpose(1, 0, 2).reshape(1, channels // 16, channels)  1.88 us
    transpose x1, local copies, waits for them, and re-layouts, on_small_slice(): grad_taps = t_sum.transpose(1, 0, 2).reshape(1, channels // 16, channels)  1.85 us
  transfers between devices with their start and end apart: 2, of which 2 were waited for; matrix products, arithmetic and copies ran while one was open for 0% of the time, Pallas kernels for 0%

profile of v2, /device:TPU:0, one launch (start us, length us, event | category | flops | bytes accessed | tf_op | source)
XLA Modules:
  0.0 82.1 jit_solution(15084383109078875316)
XLA Ops:
  0.7 1.2 %copy.18 = bf16[1,128,576]{2,1,0:T(8,128)(2,1)S(1)} copy(bf16[1,128,576]{1,2,0:T(8,128)(2,1)} %param.5) | data formatting | bytes 294912 | tf_op args[0]
  1.8 1.1 %copy.19 = bf16[1,128,576]{2,1,0:T(8,128)(2,1)S(1)} copy(bf16[1,128,576]{1,2,0:T(8,128)(2,1)} %param.9) | data formatting | bytes 294912 | tf_op args[4]
  2.9 4.1 %collective-permute-start = (bf16[2,64,576]{2,1,0:T(8,128)(2,1)S(1)}, bf16[2,64,576]{2,1,0:T(8,128)(2,1)S(1)}, u32[]{:S(2)}, u32[]{:S(2)}) collective-permute-start(bf16[2,64,576]{2,1,0:T(8,128)(2,1)S(1)} %broadcast_select_fusion), channel_id=1, source_target_pairs={{0,4},{1,5},{2,6},{3,7},{4,0},{5,1},{6,2},{7,3},{8,12},{9,13},{10,... | collective-permute-start | bytes 442376 | tf_op jit(solution)/shard_map/ppermute | solution.py:325
  7.0 7.7 %collective-permute-done = bf16[2,64,576]{2,1,0:T(8,128)(2,1)S(1)} collective-permute-done((bf16[2,64,576]{2,1,0:T(8,128)(2,1)S(1)}, bf16[2,64,576]{2,1,0:T(8,128)(2,1)S(1)}, u32[]{:S(2)}, u32[]{:S(2)}) %collective-permute-start) | collective-permute-done | bytes 147488 | tf_op jit(solution)/shard_map/ppermute | solution.py:325
  15.0 1.6 %collective-permute-done.1 = bf16[2,2,64,576]{3,2,1,0:T(8,128)(2,1)S(1)} collective-permute-done((bf16[2,2,64,576]{3,2,1,0:T(8,128)(2,1)S(1)}, bf16[2,2,64,576]{3,2,1,0:T(8,128)(2,1)S(1)}, u32[]{:S(2)}, u32[]{:S(2)}) %collective-permute-start.1) | collective-permute-done | bytes 294944 | tf_op jit(solution)/shard_map/ppermute | solution.py:328
  16.8 0.6 convolution_convert_fusion.3
  17.4 1.6 %copy-done.5 = bf16[1,2048,1024]{2,1,0:T(8,128)(2,1)S(1)} copy-done((bf16[1,2048,1024]{2,1,0:T(8,128)(2,1)S(1)}, bf16[1,2048,1024]{2,1,0:T(8,128)(2,1)}, u32[]{:S(2)}) %copy-start.5) | copy-done | bytes 4194328
  19.0 0.4 fusion.2
  19.4 0.6 fusion.48
  20.0 0.9 %add_convert_fusion = (bf16[256,1024]{1,0:T(8,128)(2,1)S(1)}, bf16[256,1024]{1,0:T(8,128)(2,1)S(1)}) fusion(bf16[256,1024]{1,0:T(8,128)(2,1)S(1)} %convolution_convert_fusion.3, f32[256,1024]{1,0:T(8,128)S(1)} %fusion.48, f32[128,1024]{1,0:T(8,128)S(1)} %fusion.2, bf16[1,2048,1024]{2,1,0:T(8,128)(2,1)S(1)} %copy-done.5), kind=kOutput, calls=%fused_computation.27 | convolution fusion | flops 538968064 | bytes 5767168 | tf_op jit(solution)/shard_map/dot_general | solution.py:20
  20.9 0.8 %fusion = f32[128,1024]{1,0:T(8,128)S(1)} fusion(bf16[1,2048,1024]{2,1,0:T(8,128)(2,1)S(1)} %copy-done.5, bf16[256,1024]{1,0:T(8,128)(2,1)S(1)} %get-tuple-element.25), kind=kOutput, calls=%fused_computation.3 | convolution fusion | flops 268435456 | bytes 2883584 | tf_op jit(solution)/shard_map/dot_general | solution.py:27
  21.8 0.7 fusion.4
  22.6 0.3 convolution_convert_fusion.1.o_ref
  22.9 0.5 fusion.30
  23.7 0.7 convolution_convert_fusion
  24.4 0.4 convolution_convert_fusion.2.i_ref
  24.8 46.8 %shard_map.84 = (f32[2,64,512]{2,1,0:T(8,128)S(1)}, bf16[576,1024]{1,0:T(8,128)(2,1)S(1)}, bf16[576,1024]{1,0:T(8,128)(2,1)S(1)}, f32[64,576]{1,0:T(8,128)S(1)}) custom-call(bf16[4,4,128,512]{3,2,1,0:T(8,128)(2,1)S(1)} %bitcast.40, bf16[576,512]{1,0:T(8,128)(2,1)S(1)} %convolution_convert_fusion.2.i_ref, ...), custom_call_target="tpu_custom_call" | custom-call | tf_op jit(solution)/shard_map/pallas_call | solution.py:294
  71.7 0.7 copy-done.1
  72.4 0.7 maximum_bitcast_fusion
  73.1 1.8 %copy.25 = f32[1,128,576]{1,2,0:T(8,128)} copy(f32[1,128,576]{2,1,0:T(8,128)} %maximum_bitcast_fusion) | data formatting | bytes 589824
  75.0 1.9 %copy.24 = f32[64,2,512]{2,1,0:T(2,128)} copy(f32[64,2,512]{2,0,1:T(8,128)} %bitcast.41) | data formatting | bytes 524288 | tf_op jit(solution)/shard_map/transpose | solution.py:365
  76.8 1.9 %reshape.15 = f32[1,64,1024]{2,1,0:T(8,128)} reshape(f32[64,2,512]{2,1,0:T(2,128)} %copy.24) | data formatting | bytes 524288 | tf_op jit(solution)/shard_map/reshape | solution.py:365
  78.7 1.7 %convert_element_type.36 = f32[576,1024]{1,0:T(8,128)} convert(bf16[576,1024]{1,0:T(8,128)(2,1)S(1)} %get-tuple-element.9) | non-fusion elementwise | flops 589824 | bytes 3538944 | tf_op jit(solution)/shard_map/convert_element_type | solution.py:366
  80.4 1.7 %convert_bitcast_fusion = f32[1024,576]{0,1:T(8,128)} fusion(bf16[576,1024]{1,0:T(8,128)(2,1)S(1)} %get-tuple-element.11), kind=kLoop, calls=%fused_computation.1 | loop fusion | flops 589824 | bytes 3538944 | tf_op jit(solution)/shard_map/transpose | solution.py:367
  (22 shorter events, 0.7 us)
Async XLA Ops:
  0.6 18.8 %copy-start = (bf16[1024,576]{0,1:T(8,128)(2,1)S(1)}, bf16[1024,576]{0,1:T(8,128)(2,1)}, u32[]{:S(2)}) copy-start(bf16[1024,576]{0,1:T(8,128)(2,1)} %param.8) | copy-start | bytes 3538948
  2.9 13.9 %copy-start.2 = (bf16[576,1024]{1,0:T(8,128)(2,1)S(1)}, bf16[576,1024]{1,0:T(8,128)(2,1)}, u32[]{:S(2)}) copy-start(bf16[576,1024]{1,0:T(8,128)(2,1)} %param.6) | copy-start | bytes 3538948
  2.9 11.8 %collective-permute-start = (bf16[2,64,576]{2,1,0:T(8,128)(2,1)S(1)}, bf16[2,64,576]{2,1,0:T(8,128)(2,1)S(1)}, u32[]{:S(2)}, u32[]{:S(2)}) collective-permute-start(bf16[2,64,576]{2,1,0:T(8,128)(2,1)S(1)} %broadcast_select_fusion), channel_id=1, source_target_pairs={{0,4},{1,5},{2,6},{3,7},{4,0},{5,1},{6,2},{7,3},{8,12},{9,13},{10,... | collective-permute-start | bytes 442376 | tf_op jit(solution)/shard_map/ppermute | solution.py:325
  14.9 1.7 %collective-permute-start.1 = (bf16[2,2,64,576]{3,2,1,0:T(8,128)(2,1)S(1)}, bf16[2,2,64,576]{3,2,1,0:T(8,128)(2,1)S(1)}, u32[]{:S(2)}, u32[]{:S(2)}) collective-permute-start(bf16[2,2,64,576]{3,2,1,0:T(8,128)(2,1)S(1)} %get-tuple-element.34), channel_id=1, source_target_pairs={{0,1},{1,0},{2,3},{3,2},{4,5},{5,4},{6,7},{7,6},{8,9},{9,8},{10,11... | collective-permute-start | bytes 884744 | tf_op jit(solution)/shard_map/ppermute | solution.py:328
  16.6 2.4 %copy-start.5 = (bf16[1,2048,1024]{2,1,0:T(8,128)(2,1)S(1)}, bf16[1,2048,1024]{2,1,0:T(8,128)(2,1)}, u32[]{:S(2)}) copy-start(bf16[1,2048,1024]{2,1,0:T(8,128)(2,1)} %param.7) | copy-start | bytes 12582916
  17.4 2.6 %copy-start.3 = (bf16[256,1024]{1,0:T(8,128)(2,1)}, bf16[256,1024]{1,0:T(8,128)(2,1)S(1)}, u32[]{:S(2)}) copy-start(bf16[256,1024]{1,0:T(8,128)(2,1)S(1)} %convolution_convert_fusion.3) | copy-start | bytes 1572868
  22.5 1.0 %copy-start.4 = (bf16[256,1024]{1,0:T(8,128)(2,1)S(1)}, bf16[256,1024]{1,0:T(8,128)(2,1)}, u32[]{:S(2)}) copy-start(bf16[256,1024]{1,0:T(8,128)(2,1)} %copy-done.3) | copy-start | bytes 1572868
  22.5 1.2 %slice-start = ((bf16[256,1024]{1,0:T(8,128)(2,1)}), bf16[128,1024]{1,0:T(8,128)(2,1)S(1)}, s32[]{:S(2)}) async-start(bf16[256,1024]{1,0:T(8,128)(2,1)} %copy-done.3), calls=%async_computation | async-start | bytes 524288 | tf_op jit(solution)/shard_map/slice | solution.py:334
  71.7 0.7 copy-start.1

commit v3 on v2

--- a/solution.py
+++ b/solution.py
@@ -99,10 +99,10 @@
 
 
 def reduce_kernel(
-    t_ref, i_ref, o_ref, p_ref,
+    t_ref, u_ref, i_ref, o_ref, p_ref,
     t_out, i_out, o_out, p_out,
-    t_r1, i_r1, o_r1, t_s2, i_s2, o_s2, t_r2, i_r2, o_r2,
-    t_z, i_z, o_z, t_rz, i_rz, o_rz, t_fin,
+    t_r1, u_r1, i_r1, o_r1, t_s2, u_s2, i_s2, o_s2, t_r2, u_r2, i_r2, o_r2,
+    t_z, u_z, i_z, o_z, t_rz, u_rz, i_rz, o_rz, t_fin, u_fin,
     send_sems, recv_sems,
 ):
     me = lax.axis_index("dp")
@@ -153,6 +153,7 @@
     io1 = (i_ref, i_r1, i_s2, i_r2, i_z, i_rz)
     oo1 = (o_ref, o_r1, o_s2, o_r2, o_z, o_rz)
     tt1 = (t_ref, t_r1, t_s2, t_r2, t_z, t_rz)
+    uu1 = (u_ref, u_r1, u_s2, u_r2, u_z, u_rz)
     tall = i_s2.shape[0]
     lanes = i_rz.shape[2]
 
@@ -220,6 +221,8 @@
     o_b = first_hop(oo1, n1, 1)
     t_a = first_hop(tt1, far, 0)
     t_b = first_hop(tt1, n1, 1)
+    u_a = first_hop(uu1, far, 0)
+    u_b = first_hop(uu1, n1, 1)
     p_copy = send(p_ref, p_out, to_z[1])
 
     arrived([i_a])
@@ -248,34 +251,46 @@
         o_part = o_out.at[rows_of(block), wide]
         return [send(i_part, i_part, peer), send(o_part, o_part, peer)]
 
+    arrived([t_b, t_2])
+    t_zs = z_hop(tt1)
+    arrived([u_a])
+    u_2 = second_hop(uu1)
+
     arrived(i_ag + o_ag)
     hop1 = forward(me, to_n1)
     hop2 = forward(me, to_n2)
     twin_me = forward(me, to_twin)
-    arrived([t_b, t_2])
-    t_zs = z_hop(tt1)
-
+    arrived([u_b, u_2])
+    u_zs = z_hop(uu1)
+
+    def finish(pack, fin, part):
+        total = z_sum(pack)
+        fin[0] = total[: total.shape[0] // 2]
+        fin[1] = total[total.shape[0] // 2 :]
+        wide = fin.shape[2]
+        cut = pl.ds(pl.multiple_of((core * 2 + part) * wide, 128), wide)
+        t_out[:, cut] = fin[core]
+        return send(fin.at[1 - core], t_out.at[:, cut], to_twin)
+
+    arrived(t_zs)
+    t_twin = finish(tt1, t_fin, 0)
     arrived(hop1)
     hop3 = forward(n1, to_n2)
     twin_n1 = forward(n1, to_twin)
     arrived(hop2)
     twin_n2 = forward(n2, to_twin)
 
-    arrived(t_zs)
-    total = z_sum(tt1)
-    t_fin[0] = total[:64]
-    t_fin[1] = total[64:]
-    t_twin = send(t_fin.at[1 - core], t_out.at[core], to_twin)
-    t_out[core] = t_fin[core]
+    arrived(u_zs)
+    u_twin = finish(uu1, u_fin, 1)
 
     arrived(hop3)
     twin_far = forward(far, to_twin)
-    arrived([t_twin, p_copy] + twin_me + twin_n1 + twin_n2 + twin_far)
+    arrived([t_twin, u_twin, p_copy] + twin_me + twin_n1 + twin_n2 + twin_far)
     for copy in made:
         copy.wait_send()
 
 
-def reduce_all(taps, inner, outer, pred):
+def reduce_all(taps, more_taps, inner, outer, pred):
     vmem = pl.BlockSpec(memory_space=pltpu.VMEM)
     t_blk = taps.shape[2:]
     features, wide = inner.shape
@@ -283,29 +298,28 @@
     scratch = []
     for lead in ((2,), (), (), ()):
         flat = pltpu.VMEM(lead + (tall, wide), BF16)
-        scratch += [pltpu.VMEM(lead + (4,) + t_blk, BF16), flat, flat]
+        blocks = pltpu.VMEM(lead + (4,) + t_blk, BF16)
+        scratch += [blocks, blocks, flat, flat]
     landing = pltpu.VMEM((3, tall, lanes), BF16)
-    scratch += [pltpu.VMEM((3,) + t_blk, BF16), landing, landing]
-    scratch += [
-        pltpu.VMEM((2, t_blk[0] // 2, t_blk[1]), F32),
-        pltpu.SemaphoreType.DMA((41,)),
-        pltpu.SemaphoreType.DMA((41,)),
-    ]
+    blocks = pltpu.VMEM((3,) + t_blk, BF16)
+    scratch += [blocks, blocks, landing, landing]
+    final = pltpu.VMEM((2, t_blk[0] // 2, t_blk[1]), F32)
+    scratch += [final, final, pltpu.SemaphoreType.DMA((48,)), pltpu.SemaphoreType.DMA((48,))]
     return pl.pallas_call(
         reduce_kernel,
         out_shape=(
-            jax.ShapeDtypeStruct((2, t_blk[0] // 2, t_blk[1]), F32),
+            jax.ShapeDtypeStruct((t_blk[0] // 2, 4 * t_blk[1]), F32),
             jax.ShapeDtypeStruct((features, 2 * wide), BF16),
             jax.ShapeDtypeStruct((features, 2 * wide), BF16),
             jax.ShapeDtypeStruct(pred.shape, F32),
         ),
-        in_specs=[vmem] * 4,
+        in_specs=[vmem] * 5,
         out_specs=[vmem] * 4,
         scratch_shapes=scratch,
         compiler_params=pltpu.CompilerParams(
             collective_id=0, has_side_effects=True, vmem_limit_bytes=24 * 1024 * 1024
         ),
-    )(taps, inner, outer, pred)
+    )(taps, more_taps, inner, outer, pred)
 
 
 def on_small_slice(wall_inputs, in_weight, tap_weights, out_weight, cotangent):
@@ -352,17 +366,20 @@
     hidden_cols = lax.dynamic_slice_in_dim(hidden_1, core * wide, wide, 1)
     lagged = jnp.concatenate([jnp.zeros_like(lag), lag])
     both = jnp.concatenate([lagged, hidden], axis=1)
-    taps = contract_rows(both, pre_cols).astype(BF16).reshape(4, 4, channels // 8, wide)
+    taps, more_taps = [
+        contract_rows(both, part).astype(BF16).reshape(4, 4, channels // 8, wide // 2)
+        for part in (pre_cols[:, : wide // 2], pre_cols[:, wide // 2 :])
+    ]
     inner = contract_rows(inputs, back_cols).astype(BF16)
     outer = contract_rows(cots, hidden_cols).astype(BF16)
 
     pred_keep = jnp.where(early, pred[:half], pred[half:])
     pred_give = jnp.where(early, pred[half:], pred[:half])
-    t_sum, i_sum, o_sum, pred_got = reduce_all(taps, inner, outer, pred_give)
+    t_sum, i_sum, o_sum, pred_got = reduce_all(taps, more_taps, inner, outer, pred_give)
     prediction = jnp.concatenate(
         [jnp.where(early, pred_keep, pred_got), jnp.where(early, pred_got, pred_keep)]
     )[None]
-    grad_taps = t_sum.transpose(1, 0, 2).reshape(1, channels // 16, channels)
+    grad_taps = t_sum[None]
     grad_in = i_sum.astype(F32)
     grad_out = o_sum.astype(F32).T
     return prediction, grad_in, grad_taps, grad_out

time: 82.7 us -> 79.3 us (0.959)
  local copies, waits for them, and re-layouts: 10.4 us -> 6.96 us
    reshape x1 -> x0, local copies, waits for them, and re-layouts: 1.88 us -> none  [on_small_slice(): grad_taps = t_sum.transpose(1, 0, 2).reshape(1, channels // 16, channels)]
    transpose x1 -> x0, local copies, waits for them, and re-layouts: 1.85 us -> none  [on_small_slice(): grad_taps = t_sum.transpose(1, 0, 2).reshape(1, channels // 16, channels)]
    unnamed x15 -> x14, local copies, waits for them, and re-layouts: 6.44 us -> 6.86 us
    dot_general x3 -> x4, matrix products: 1.42 us -> 1.68 us  [contract_rows(): lax.dot_general(left.reshape(-1, left.shape[-1]), right.reshape(-1, right...]
where the time goes in v3:
time: 79.3 us; the launch traced here: 79.1 us
  Pallas kernels  47 us (59%)
  waiting for transfers between devices  9.31 us (12%)
  local copies, waits for them, and re-layouts  6.96 us (9%)
  matrix products  6.28 us (8%)
  other arithmetic  4.46 us (6%)
  starting transfers between devices  4.17 us (5%)
  between operations  0.86 us (1%)
    pallas_call x1, Pallas kernels, reduce_all(): pl.pallas_call(reduce_kernel, out_shape=(jax.ShapeDtypeStruct((t_blk[0] /...  47 us
    ppermute x1, waiting for transfers between devices, on_small_slice(): lax.ppermute(give, 'tm', [(i, (i + shards // 2) % shards) for i in range(...  7.71 us
    unnamed x14, local copies, waits for them, and re-layouts  6.86 us
    ppermute x1, starting transfers between devices, on_small_slice(): lax.ppermute(give, 'tm', [(i, (i + shards // 2) % shards) for i in range(...  4.1 us
    dot_general x4, matrix products, project(): jnp.dot(rows, weight, preferred_element_type=jnp.float32)  2.44 us
    dot_general x3, matrix products, project_back(): lax.dot_general(rows, weight, (((1,), (1,)), ((), ())), preferred_element...  2.15 us
    convert_element_type x1, other arithmetic, on_small_slice(): grad_in = i_sum.astype(F32)  1.69 us
    transpose x1, other arithmetic, on_small_slice(): grad_out = o_sum.astype(F32).T  1.69 us
  transfers between devices with their start and end apart: 2, of which 2 were waited for; matrix products, arithmetic and copies ran while one was open for 0% of the time, Pallas kernels for 0%

profile of v3, /device:TPU:0, one launch (start us, length us, event | category | flops | bytes accessed | tf_op | source)
XLA Modules:
  0.0 79.1 jit_solution(12024328661083544621)
XLA Ops:
  0.7 1.2 %copy.18 = bf16[1,128,576]{2,1,0:T(8,128)(2,1)S(1)} copy(bf16[1,128,576]{1,2,0:T(8,128)(2,1)} %param.9) | data formatting | bytes 294912 | tf_op args[4]
  1.8 1.1 %copy.17 = bf16[1,128,576]{2,1,0:T(8,128)(2,1)S(1)} copy(bf16[1,128,576]{1,2,0:T(8,128)(2,1)} %param.5) | data formatting | bytes 294912 | tf_op args[0]
  2.9 4.1 %collective-permute-start = (bf16[2,64,576]{2,1,0:T(8,128)(2,1)S(1)}, bf16[2,64,576]{2,1,0:T(8,128)(2,1)S(1)}, u32[]{:S(2)}, u32[]{:S(2)}) collective-permute-start(bf16[2,64,576]{2,1,0:T(8,128)(2,1)S(1)} %broadcast_select_fusion), channel_id=1, source_target_pairs={{0,4},{1,5},{2,6},{3,7},{4,0},{5,1},{6,2},{7,3},{8,12},{9,13},{10,... | collective-permute-start | bytes 442376 | tf_op jit(solution)/shard_map/ppermute | solution.py:339
  7.0 7.7 %collective-permute-done = bf16[2,64,576]{2,1,0:T(8,128)(2,1)S(1)} collective-permute-done((bf16[2,64,576]{2,1,0:T(8,128)(2,1)S(1)}, bf16[2,64,576]{2,1,0:T(8,128)(2,1)S(1)}, u32[]{:S(2)}, u32[]{:S(2)}) %collective-permute-start) | collective-permute-done | bytes 147488 | tf_op jit(solution)/shard_map/ppermute | solution.py:339
  15.0 1.6 %collective-permute-done.1 = bf16[2,2,64,576]{3,2,1,0:T(8,128)(2,1)S(1)} collective-permute-done((bf16[2,2,64,576]{3,2,1,0:T(8,128)(2,1)S(1)}, bf16[2,2,64,576]{3,2,1,0:T(8,128)(2,1)S(1)}, u32[]{:S(2)}, u32[]{:S(2)}) %collective-permute-start.1) | collective-permute-done | bytes 294944 | tf_op jit(solution)/shard_map/ppermute | solution.py:342
  16.8 0.6 convolution_convert_fusion.4
  17.4 1.4 %copy-done.4 = bf16[1,2048,1024]{2,1,0:T(8,128)(2,1)S(1)} copy-done((bf16[1,2048,1024]{2,1,0:T(8,128)(2,1)S(1)}, bf16[1,2048,1024]{2,1,0:T(8,128)(2,1)}, u32[]{:S(2)}) %copy-start.4) | copy-done | bytes 4194328
  18.8 0.4 fusion.2
  19.3 0.6 fusion.52
  19.8 0.9 %add_convert_fusion = (bf16[256,1024]{1,0:T(8,128)(2,1)S(1)}, bf16[256,1024]{1,0:T(8,128)(2,1)S(1)}) fusion(bf16[256,1024]{1,0:T(8,128)(2,1)S(1)} %convolution_convert_fusion.4, f32[256,1024]{1,0:T(8,128)S(1)} %fusion.52, f32[128,1024]{1,0:T(8,128)S(1)} %fusion.2, bf16[1,2048,1024]{2,1,0:T(8,128)(2,1)S(1)} %copy-done.4), kind=kOutput, calls=%fused_computation.25 | convolution fusion | flops 538968064 | bytes 5767168 | tf_op jit(solution)/shard_map/dot_general | solution.py:20
  20.7 0.8 %fusion = f32[128,1024]{1,0:T(8,128)S(1)} fusion(bf16[1,2048,1024]{2,1,0:T(8,128)(2,1)S(1)} %copy-done.4, bf16[256,1024]{1,0:T(8,128)(2,1)S(1)} %get-tuple-element.25), kind=kOutput, calls=%fused_computation.4 | convolution fusion | flops 268435456 | bytes 2883584 | tf_op jit(solution)/shard_map/dot_general | solution.py:27
  21.6 0.7 fusion.4
  22.3 0.3 convolution_convert_fusion.2.o_ref
  22.7 0.5 convolution_convert_fusion.1
  23.2 0.5 convolution_convert_fusion
  23.7 0.5 fusion.29
  24.2 0.4 convolution_convert_fusion.3.i_ref
  24.6 47.0 %shard_map.84 = (f32[64,1024]{1,0:T(8,128)S(1)}, bf16[576,1024]{1,0:T(8,128)(2,1)S(1)}, bf16[576,1024]{1,0:T(8,128)(2,1)S(1)}, f32[64,576]{1,0:T(8,128)S(1)}) custom-call(bf16[4,4,128,256]{3,2,1,0:T(8,128)(2,1)S(1)} %bitcast.41, bf16[4,4,128,256]{3,2,1,0:T(8,128)(2,1)S(1)} %bitcast.42, bf16[576,512]{1,0:T(8,128)(2,1)S(1)} %convolution_convert_fusion.3.i_ref, ...), custom_call_target="tpu_custom_call" | custom-call | tf_op jit(solution)/shard_map/pallas_call | solution.py:308
  71.7 0.7 copy-done.1
  72.4 0.7 maximum_bitcast_fusion
  73.1 1.8 %copy.23 = f32[1,128,576]{1,2,0:T(8,128)} copy(f32[1,128,576]{2,1,0:T(8,128)} %maximum_bitcast_fusion) | data formatting | bytes 589824
  75.0 1.7 %convert_element_type.40 = f32[576,1024]{1,0:T(8,128)} convert(bf16[576,1024]{1,0:T(8,128)(2,1)S(1)} %get-tuple-element.9) | non-fusion elementwise | flops 589824 | bytes 3538944 | tf_op jit(solution)/shard_map/convert_element_type | solution.py:383
  76.7 1.7 %convert_bitcast_fusion = f32[1024,576]{0,1:T(8,128)} fusion(bf16[576,1024]{1,0:T(8,128)(2,1)S(1)} %get-tuple-element.11), kind=kLoop, calls=%fused_computation.2 | loop fusion | flops 589824 | bytes 3538944 | tf_op jit(solution)/shard_map/transpose | solution.py:384
  78.4 0.7 copy.26
  (19 shorter events, 0.5 us)
Async XLA Ops:
  0.6 18.6 %copy-start = (bf16[1024,576]{0,1:T(8,128)(2,1)S(1)}, bf16[1024,576]{0,1:T(8,128)(2,1)}, u32[]{:S(2)}) copy-start(bf16[1024,576]{0,1:T(8,128)(2,1)} %param.8) | copy-start | bytes 3538948
  2.9 13.9 %copy-start.3 = (bf16[576,1024]{1,0:T(8,128)(2,1)S(1)}, bf16[576,1024]{1,0:T(8,128)(2,1)}, u32[]{:S(2)}) copy-start(bf16[576,1024]{1,0:T(8,128)(2,1)} %param.6) | copy-start | bytes 3538948
  2.9 11.8 %collective-permute-start = (bf16[2,64,576]{2,1,0:T(8,128)(2,1)S(1)}, bf16[2,64,576]{2,1,0:T(8,128)(2,1)S(1)}, u32[]{:S(2)}, u32[]{:S(2)}) collective-permute-start(bf16[2,64,576]{2,1,0:T(8,128)(2,1)S(1)} %broadcast_select_fusion), channel_id=1, source_target_pairs={{0,4},{1,5},{2,6},{3,7},{4,0},{5,1},{6,2},{7,3},{8,12},{9,13},{10,... | collective-permute-start | bytes 442376 | tf_op jit(solution)/shard_map/ppermute | solution.py:339
  14.9 1.7 %collective-permute-start.1 = (bf16[2,2,64,576]{3,2,1,0:T(8,128)(2,1)S(1)}, bf16[2,2,64,576]{3,2,1,0:T(8,128)(2,1)S(1)}, u32[]{:S(2)}, u32[]{:S(2)}) collective-permute-start(bf16[2,2,64,576]{3,2,1,0:T(8,128)(2,1)S(1)} %get-tuple-element.34), channel_id=1, source_target_pairs={{0,1},{1,0},{2,3},{3,2},{4,5},{5,4},{6,7},{7,6},{8,9},{9,8},{10,11... | collective-permute-start | bytes 884744 | tf_op jit(solution)/shard_map/ppermute | solution.py:342
  16.6 2.2 %copy-start.4 = (bf16[1,2048,1024]{2,1,0:T(8,128)(2,1)S(1)}, bf16[1,2048,1024]{2,1,0:T(8,128)(2,1)}, u32[]{:S(2)}) copy-start(bf16[1,2048,1024]{2,1,0:T(8,128)(2,1)} %param.7) | copy-start | bytes 12582916
  71.7 0.7 copy-start.1
  76.7 1.7 %copy-start.2 = (f32[64,1024]{1,0:T(8,128)S(1)}, f32[64,1024]{1,0:T(8,128)}, u32[]{:S(2)}) copy-start(f32[64,1024]{1,0:T(8,128)} %copy-done.1) | copy-start | bytes 786436

commit v4 on v3

--- a/solution.py
+++ b/solution.py
@@ -102,7 +102,7 @@
     t_ref, u_ref, i_ref, o_ref, p_ref,
     t_out, i_out, o_out, p_out,
     t_r1, u_r1, i_r1, o_r1, t_s2, u_s2, i_s2, o_s2, t_r2, u_r2, i_r2, o_r2,
-    t_z, u_z, i_z, o_z, t_rz, u_rz, i_rz, o_rz, t_fin, u_fin,
+    t_z, u_z, i_z, o_z, t_rz, u_rz, i_rz, o_rz, t_fin, u_fin, p_buf,
     send_sems, recv_sems,
 ):
     me = lax.axis_index("dp")
@@ -223,7 +223,12 @@
     t_b = first_hop(tt1, n1, 1)
     u_a = first_hop(uu1, far, 0)
     u_b = first_hop(uu1, n1, 1)
-    p_copy = send(p_ref, p_out, to_z[1])
+    half = p_ref.shape[0] // 2
+    late = tm // 4
+    kept = pl.ds(pl.multiple_of(late * half, 8), half)
+    given = pl.ds(pl.multiple_of((1 - late) * half, 8), half)
+    p_copy = send(p_ref.at[given], p_buf.at[kept], to_z[1])
+    p_buf[kept] = p_ref[kept]
 
     arrived([i_a])
     i_2 = second_hop(io1)
@@ -272,6 +277,9 @@
         t_out[:, cut] = fin[core]
         return send(fin.at[1 - core], t_out.at[:, cut], to_twin)
 
+    arrived([p_copy])
+    p_out[...] = p_buf[...].T
+
     arrived(t_zs)
     t_twin = finish(tt1, t_fin, 0)
     arrived(hop1)
@@ -285,7 +293,7 @@
 
     arrived(hop3)
     twin_far = forward(far, to_twin)
-    arrived([t_twin, u_twin, p_copy] + twin_me + twin_n1 + twin_n2 + twin_far)
+    arrived([t_twin, u_twin] + twin_me + twin_n1 + twin_n2 + twin_far)
     for copy in made:
         copy.wait_send()
 
@@ -304,14 +312,15 @@
     blocks = pltpu.VMEM((3,) + t_blk, BF16)
     scratch += [blocks, blocks, landing, landing]
     final = pltpu.VMEM((2, t_blk[0] // 2, t_blk[1]), F32)
-    scratch += [final, final, pltpu.SemaphoreType.DMA((48,)), pltpu.SemaphoreType.DMA((48,))]
+    scratch += [final, final, pltpu.VMEM(pred.shape, F32)]
+    scratch += [pltpu.SemaphoreType.DMA((48,)), pltpu.SemaphoreType.DMA((48,))]
     return pl.pallas_call(
         reduce_kernel,
         out_shape=(
             jax.ShapeDtypeStruct((t_blk[0] // 2, 4 * t_blk[1]), F32),
             jax.ShapeDtypeStruct((features, 2 * wide), BF16),
             jax.ShapeDtypeStruct((features, 2 * wide), BF16),
-            jax.ShapeDtypeStruct(pred.shape, F32),
+            jax.ShapeDtypeStruct(pred.shape[::-1], F32),
         ),
         in_specs=[vmem] * 5,
         out_specs=[vmem] * 4,
@@ -322,27 +331,78 @@
     )(taps, more_taps, inner, outer, pred)
 
 
+def pair_kernel(x_ref, c_ref, x_out, c_out, send_sems, recv_sems):
+    me = lax.axis_index("dp")
+    tm = lax.axis_index("tm")
+    z, core = tm // 2, tm % 2
+    late = tm // 4
+    mesh_ids = pl.DeviceIdType.MESH
+    peer = {"dp": me, "tm": ((z + 2) % 4) * 2 + core}
+    twin = {"dp": me, "tm": z * 2 + 1 - core}
+    half = x_ref.shape[0] // 2
+
+    def cut(at):
+        return pl.ds(pl.multiple_of(at * half, 16), half)
+
+    barrier = pltpu.get_barrier_semaphore()
+    for other in (peer, twin):
+        pl.semaphore_signal(barrier, inc=1, device_id=other, device_id_type=mesh_ids)
+    pl.semaphore_wait(barrier, 2)
+
+    def send(at, src, dst, to):
+        copy = pltpu.make_async_remote_copy(
+            src_ref=src, dst_ref=dst, send_sem=send_sems.at[at], recv_sem=recv_sems.at[at],
+            device_id=to, device_id_type=mesh_ids,
+        )
+        copy.start()
+        return copy
+
+    pairs = ((x_ref, x_out), (c_ref, c_out))
+    far = [
+        send(k, src.at[cut(1 - late)], out.at[cut(2 * late)], peer)
+        for k, (src, out) in enumerate(pairs)
+    ]
+    near = [
+        send(2 + k, src.at[cut(late)], out.at[cut(2 * late + 1)], twin)
+        for k, (src, out) in enumerate(pairs)
+    ]
+    for src, out in pairs:
+        out[cut(2 * late)] = src[cut(late)]
+    for k, (_, out) in enumerate(pairs):
+        far[k].wait_recv()
+        got = 2 * (1 - late)
+        near.append(send(4 + k, out.at[cut(got)], out.at[cut(got + 1)], twin))
+    for copy in near:
+        copy.wait_recv()
+    for copy in far + near:
+        copy.wait_send()
+
+
+def pair_rows(x, c):
+    vmem = pl.BlockSpec(memory_space=pltpu.VMEM)
+    rows, features = x.shape
+    return pl.pallas_call(
+        pair_kernel,
+        out_shape=(jax.ShapeDtypeStruct((2 * rows, features), BF16),) * 2,
+        in_specs=[vmem] * 2,
+        out_specs=[vmem] * 2,
+        scratch_shapes=[pltpu.SemaphoreType.DMA((6,)), pltpu.SemaphoreType.DMA((6,))],
+        compiler_params=pltpu.CompilerParams(
+            collective_id=1, has_side_effects=True, vmem_limit_bytes=8 * 1024 * 1024
+        ),
+    )(x, c)
+
+
 def on_small_slice(wall_inputs, in_weight, tap_weights, out_weight, cotangent):
     channels = tap_weights.shape[2]
     wide = channels // 2
     rows, features = wall_inputs.shape[1:]
     half = rows // 2
     tm = lax.axis_index("tm")
-    shards = lax.axis_size("tm")
-    early = tm < shards // 2
     core = tm % 2
     delayed_w, current_w = tap_weights[0, :channels], tap_weights[0, channels:]
 
-    local = jnp.stack([wall_inputs[0], cotangent[0]])
-    keep = jnp.where(early, local[:, :half], local[:, half:])
-    give = jnp.where(early, local[:, half:], local[:, :half])
-    got = lax.ppermute(give, "tm", [(i, (i + shards // 2) % shards) for i in range(shards)])
-    low, high = jnp.where(early, keep, got), jnp.where(early, got, keep)
-    pairs = jnp.stack([low, high])
-    twin = lax.ppermute(pairs, "tm", [(i, i + 1 - 2 * (i % 2)) for i in range(shards)])
-    everything = jnp.stack([pairs, twin], axis=1)
-    inputs = everything[:, :, 0].reshape(4 * half, features)
-    cots = everything[:, :, 1].reshape(4 * half, features)
+    inputs, cots = pair_rows(wall_inputs[0], cotangent[0])
 
     hidden = project(inputs, in_weight).astype(BF16)
     lag = hidden[: 2 * half]
@@ -373,12 +433,8 @@
     inner = contract_rows(inputs, back_cols).astype(BF16)
     outer = contract_rows(cots, hidden_cols).astype(BF16)
 
-    pred_keep = jnp.where(early, pred[:half], pred[half:])
-    pred_give = jnp.where(early, pred[half:], pred[:half])
-    t_sum, i_sum, o_sum, pred_got = reduce_all(taps, more_taps, inner, outer, pred_give)
-    prediction = jnp.concatenate(
-        [jnp.where(early, pred_keep, pred_got), jnp.where(early, pred_got, pred_keep)]
-    )[None]
+    t_sum, i_sum, o_sum, pred_sum = reduce_all(taps, more_taps, inner, outer, pred)
+    prediction = pred_sum.T[None]
     grad_taps = t_sum[None]
     grad_in = i_sum.astype(F32)
     grad_out = o_sum.astype(F32).T

time: 79.3 us -> 78.7 us (level)
  Pallas kernels: 47 us -> 59.5 us
  waiting for transfers between devices: 9.31 us -> 0 us
  matrix products: 6.28 us -> 11.1 us
  starting transfers between devices: 4.17 us -> 0 us
  local copies, waits for them, and re-layouts: 6.96 us -> 3.75 us
  other arithmetic: 4.46 us -> 3.38 us
    pallas_call x0 -> x1, Pallas kernels: none -> 13.5 us  [pair_rows(): pl.pallas_call(pair_kernel, out_shape=(jax.ShapeDtypeStruct((2 * rows, fe...]
    ppermute x2 -> x0, waiting for transfers between devices: 9.31 us -> none  [the longest x1 7.71 us: on_small_slice(): lax.ppermute(give, 'tm', [(i, (i + shards // 2) % shards) for i in range(...]
    ppermute x2 -> x0, starting transfers between devices: 4.17 us -> none  [the longest x1 4.1 us: on_small_slice(): lax.ppermute(give, 'tm', [(i, (i + shards // 2) % shards) for i in range(...]
    unnamed x14 -> x10, local copies, waits for them, and re-layouts: 6.86 us -> 3.71 us
    dot_general x4, matrix products: 2.44 us -> 5.47 us  [project(): jnp.dot(rows, weight, preferred_element_type=jnp.float32)]
    dot_general x4, matrix products: 1.68 us -> 3.49 us  [contract_rows(): lax.dot_general(left.reshape(-1, left.shape[-1]), right.reshape(-1, right...]
    pallas_call x1, Pallas kernels: 47 us -> 46 us  [reduce_all(): pl.pallas_call(reduce_kernel, out_shape=(jax.ShapeDtypeStruct((t_blk[0] /...]
  transfers between devices with their start and end apart: 2 -> 0, of which waited for: 2 -> 0; matrix products, arithmetic and copies ran while one was open for 0% -> 0% of each run, Pallas kernels for 0% -> 0%
where the time goes in v4:
time: 78.7 us; the launch traced here: 78.5 us
  Pallas kernels  59.5 us (76%)
  matrix products  11.1 us (14%)
  local copies, waits for them, and re-layouts  3.75 us (5%)
  other arithmetic  3.38 us (4%)
  between operations  0.79 us (1%)
    pallas_call x1, Pallas kernels, reduce_all(): pl.pallas_call(reduce_kernel, out_shape=(jax.ShapeDtypeStruct((t_blk[0] /...  46 us
    pallas_call x1, Pallas kernels, pair_rows(): pl.pallas_call(pair_kernel, out_shape=(jax.ShapeDtypeStruct((2 * rows, fe...  13.5 us
    dot_general x4, matrix products, project(): jnp.dot(rows, weight, preferred_element_type=jnp.float32)  5.47 us
    unnamed x10, local copies, waits for them, and re-layouts  3.71 us
    dot_general x4, matrix products, contract_rows(): lax.dot_general(left.reshape(-1, left.shape[-1]), right.reshape(-1, right...  3.49 us
    dot_general x3, matrix products, project_back(): lax.dot_general(rows, weight, (((1,), (1,)), ((), ())), preferred_element...  2.14 us
    transpose x1, other arithmetic, on_small_slice(): grad_out = o_sum.astype(F32).T  1.69 us
    convert_element_type x1, other arithmetic, on_small_slice(): grad_in = i_sum.astype(F32)  1.69 us

profile of v4, /device:TPU:0, one launch (start us, length us, event | category | flops | bytes accessed | tf_op | source)
XLA Modules:
  0.0 78.5 jit_solution(12432504294332150171)
XLA Ops:
  0.6 0.0 copy-start
  0.7 1.2 %copy.9 = bf16[1,128,576]{2,1,0:T(8,128)(2,1)S(1)} copy(bf16[1,128,576]{1,2,0:T(8,128)(2,1)} %param.5) | data formatting | bytes 294912 | tf_op args[0]
  1.8 1.1 %copy.10 = bf16[1,128,576]{2,1,0:T(8,128)(2,1)S(1)} copy(bf16[1,128,576]{1,2,0:T(8,128)(2,1)} %param.9) | data formatting | bytes 294912 | tf_op args[4]
  2.9 13.5 %shard_map.84 = (bf16[256,576]{1,0:T(8,128)(2,1)S(1)}, bf16[256,576]{1,0:T(8,128)(2,1)S(1)}) custom-call(bf16[128,576]{1,0:T(8,128)(2,1)S(1)} %bitcast.37, bf16[128,576]{1,0:T(8,128)(2,1)S(1)} %bitcast.38), custom_call_target="tpu_custom_call" | custom-call | tf_op jit(solution)/shard_map/pallas_call | solution.py:384
  16.4 1.9 %convolution_convert_fusion.4 = bf16[256,1024]{1,0:T(8,128)(2,1)S(1)} fusion(bf16[256,576]{1,0:T(8,128)(2,1)S(1)} %get-tuple-element.10, bf16[576,1024]{1,0:T(8,128)(2,1)} %param.6), kind=kOutput, calls=%fused_computation.21 | convolution fusion | flops 302252032 | bytes 1998848 | tf_op jit(solution)/shard_map/dot_general | solution.py:20
  18.2 0.0 copy-start.1
  18.3 2.2 %fusion.2 = f32[128,1024]{1,0:T(8,128)S(1)} fusion(bf16[1,2048,1024]{2,1,0:T(8,128)(2,1)} %param.7, bf16[256,1024]{1,0:T(8,128)(2,1)S(1)} %convolution_convert_fusion.4), kind=kOutput, calls=%fused_computation.6 | convolution fusion | flops 268435456 | bytes 2883584 | tf_op jit(solution)/shard_map/dot_general | solution.py:20
  20.5 0.6 fusion.49
  21.0 0.0 copy-done.1
  21.1 0.9 %add_convert_fusion = (bf16[256,1024]{1,0:T(8,128)(2,1)S(1)}, bf16[256,1024]{1,0:T(8,128)(2,1)S(1)}) fusion(bf16[256,1024]{1,0:T(8,128)(2,1)S(1)} %convolution_convert_fusion.4, f32[256,1024]{1,0:T(8,128)S(1)} %fusion.49, f32[128,1024]{1,0:T(8,128)S(1)} %fusion.2, bf16[1,2048,1024]{2,1,0:T(8,128)(2,1)S(1)} %copy-done.1), kind=kOutput, calls=%fused_computation.23 | convolution fusion | flops 538968064 | bytes 5767168 | tf_op jit(solution)/shard_map/dot_general | solution.py:20
  22.0 0.0 copy-start.2
  22.0 0.7 fusion.4
  22.7 0.0 copy-done.2
  22.8 0.8 %fusion = f32[128,1024]{1,0:T(8,128)S(1)} fusion(bf16[1,2048,1024]{2,1,0:T(8,128)(2,1)S(1)} %copy-done.1, bf16[256,1024]{1,0:T(8,128)(2,1)S(1)} %get-tuple-element.17), kind=kOutput, calls=%fused_computation.4 | convolution fusion | flops 268435456 | bytes 2883584 | tf_op jit(solution)/shard_map/dot_general | solution.py:27
  23.6 0.4 convolution_convert_fusion.3.i_ref
  24.0 1.4 %convolution_convert_fusion = bf16[2048,256]{1,0:T(8,128)(2,1)S(1)} fusion(bf16[128,1024]{1,0:T(8,128)(2,1)S(1)} %slice.32, bf16[256,1024]{1,0:T(8,128)(2,1)S(1)} %convolution_convert_fusion.4, bf16[256,1024]{1,0:T(8,128)(2,1)} %copy-done.2, s32[]{:T(128)S(6)} %add.33), kind=kOutput, calls=%fused_computation | convolution fusion | flops 272105472 | bytes 1966084 | tf_op jit(solution)/shard_map/dot_general | solution.py:34
  25.4 0.3 convolution_convert_fusion.2.o_ref
  25.8 1.4 %convolution_convert_fusion.1 = bf16[2048,256]{1,0:T(8,128)(2,1)S(1)} fusion(bf16[128,1024]{1,0:T(8,128)(2,1)S(1)} %slice.32, bf16[256,1024]{1,0:T(8,128)(2,1)S(1)} %convolution_convert_fusion.4, bf16[256,1024]{1,0:T(8,128)(2,1)} %copy-done.2, s32[]{:T(128)S(6)} %select_n.13), kind=kOutput, calls=%fused_computation.1 | convolution fusion | flops 272105472 | bytes 1966084 | tf_op jit(solution)/shard_map/dot_general | solution.py:34
  27.2 0.5 fusion.28.p_ref
  27.7 46.0 %shard_map.85 = (f32[64,1024]{1,0:T(8,128)S(1)}, bf16[576,1024]{1,0:T(8,128)(2,1)S(1)}, bf16[576,1024]{1,0:T(8,128)(2,1)S(1)}, f32[576,128]{1,0:T(8,128)S(1)}) custom-call(bf16[4,4,128,256]{3,2,1,0:T(8,128)(2,1)S(1)} %bitcast.36, bf16[4,4,128,256]{3,2,1,0:T(8,128)(2,1)S(1)} %bitcast.35, bf16[576,512]{1,0:T(8,128)(2,1)S(1)} %convolution_convert_fusion.3.i_ref, ...), custom_call_target="tpu_custom_call" | custom-call | tf_op jit(solution)/shard_map/pallas_call | solution.py:317
  73.7 1.7 %convert_bitcast_fusion = f32[1024,576]{0,1:T(8,128)} fusion(bf16[576,1024]{1,0:T(8,128)(2,1)S(1)} %get-tuple-element.15), kind=kLoop, calls=%fused_computation.2 | loop fusion | flops 589824 | bytes 3538944 | tf_op jit(solution)/shard_map/transpose | solution.py:440
  75.4 1.7 %convert_element_type.40 = f32[576,1024]{1,0:T(8,128)} convert(bf16[576,1024]{1,0:T(8,128)(2,1)S(1)} %get-tuple-element.13) | non-fusion elementwise | flops 589824 | bytes 3538944 | tf_op jit(solution)/shard_map/convert_element_type | solution.py:439
  77.1 0.7 copy.15
  77.8 0.7 copy.16
  (3 shorter events, 0.0 us)
Async XLA Ops:
  0.6 19.8 %copy-start = (bf16[1024,576]{0,1:T(8,128)(2,1)S(1)}, bf16[1024,576]{0,1:T(8,128)(2,1)}, u32[]{:S(2)}) copy-start(bf16[1024,576]{0,1:T(8,128)(2,1)} %param.8) | copy-start | bytes 3538948
  18.2 2.8 %copy-start.1 = (bf16[1,2048,1024]{2,1,0:T(8,128)(2,1)S(1)}, bf16[1,2048,1024]{2,1,0:T(8,128)(2,1)}, u32[]{:S(2)}) copy-start(bf16[1,2048,1024]{2,1,0:T(8,128)(2,1)} %param.7) | copy-start | bytes 12582916
  22.0 0.8 %copy-start.2 = (bf16[256,1024]{1,0:T(8,128)(2,1)}, bf16[256,1024]{1,0:T(8,128)(2,1)S(1)}, u32[]{:S(2)}) copy-start(bf16[256,1024]{1,0:T(8,128)(2,1)S(1)} %get-tuple-element.17) | copy-start | bytes 1572868

commit v5 on v3

--- a/solution.py
+++ b/solution.py
@@ -102,7 +102,7 @@
     t_ref, u_ref, i_ref, o_ref, p_ref,
     t_out, i_out, o_out, p_out,
     t_r1, u_r1, i_r1, o_r1, t_s2, u_s2, i_s2, o_s2, t_r2, u_r2, i_r2, o_r2,
-    t_z, u_z, i_z, o_z, t_rz, u_rz, i_rz, o_rz, t_fin, u_fin,
+    t_z, u_z, i_z, o_z, t_rz, u_rz, i_rz, o_rz, t_fin, u_fin, p_buf,
     send_sems, recv_sems,
 ):
     me = lax.axis_index("dp")
@@ -223,7 +223,12 @@
     t_b = first_hop(tt1, n1, 1)
     u_a = first_hop(uu1, far, 0)
     u_b = first_hop(uu1, n1, 1)
-    p_copy = send(p_ref, p_out, to_z[1])
+    half = p_ref.shape[0] // 2
+    late = tm // 4
+    kept = pl.ds(pl.multiple_of(late * half, 8), half)
+    given = pl.ds(pl.multiple_of((1 - late) * half, 8), half)
+    p_copy = send(p_ref.at[given], p_buf.at[kept], to_z[1])
+    p_buf[kept] = p_ref[kept]
 
     arrived([i_a])
     i_2 = second_hop(io1)
@@ -272,6 +277,9 @@
         t_out[:, cut] = fin[core]
         return send(fin.at[1 - core], t_out.at[:, cut], to_twin)
 
+    arrived([p_copy])
+    p_out[...] = p_buf[...].T
+
     arrived(t_zs)
     t_twin = finish(tt1, t_fin, 0)
     arrived(hop1)
@@ -285,7 +293,7 @@
 
     arrived(hop3)
     twin_far = forward(far, to_twin)
-    arrived([t_twin, u_twin, p_copy] + twin_me + twin_n1 + twin_n2 + twin_far)
+    arrived([t_twin, u_twin] + twin_me + twin_n1 + twin_n2 + twin_far)
     for copy in made:
         copy.wait_send()
 
@@ -304,14 +312,15 @@
     blocks = pltpu.VMEM((3,) + t_blk, BF16)
     scratch += [blocks, blocks, landing, landing]
     final = pltpu.VMEM((2, t_blk[0] // 2, t_blk[1]), F32)
-    scratch += [final, final, pltpu.SemaphoreType.DMA((48,)), pltpu.SemaphoreType.DMA((48,))]
+    scratch += [final, final, pltpu.VMEM(pred.shape, F32)]
+    scratch += [pltpu.SemaphoreType.DMA((48,)), pltpu.SemaphoreType.DMA((48,))]
     return pl.pallas_call(
         reduce_kernel,
         out_shape=(
             jax.ShapeDtypeStruct((t_blk[0] // 2, 4 * t_blk[1]), F32),
             jax.ShapeDtypeStruct((features, 2 * wide), BF16),
             jax.ShapeDtypeStruct((features, 2 * wide), BF16),
-            jax.ShapeDtypeStruct(pred.shape, F32),
+            jax.ShapeDtypeStruct(pred.shape[::-1], F32),
         ),
         in_specs=[vmem] * 5,
         out_specs=[vmem] * 4,
@@ -373,12 +382,8 @@
     inner = contract_rows(inputs, back_cols).astype(BF16)
     outer = contract_rows(cots, hidden_cols).astype(BF16)
 
-    pred_keep = jnp.where(early, pred[:half], pred[half:])
-    pred_give = jnp.where(early, pred[half:], pred[:half])
-    t_sum, i_sum, o_sum, pred_got = reduce_all(taps, more_taps, inner, outer, pred_give)
-    prediction = jnp.concatenate(
-        [jnp.where(early, pred_keep, pred_got), jnp.where(early, pred_got, pred_keep)]
-    )[None]
+    t_sum, i_sum, o_sum, pred_sum = reduce_all(taps, more_taps, inner, outer, pred)
+    prediction = pred_sum.T[None]
     grad_taps = t_sum[None]
     grad_in = i_sum.astype(F32)
     grad_out = o_sum.astype(F32).T

time: 79.3 us -> 76.7 us (0.967)
  local copies, waits for them, and re-layouts: 6.96 us -> 5.16 us
    unnamed x14 -> x10, local copies, waits for them, and re-layouts: 6.86 us -> 5.06 us
where the time goes in v5:
time: 76.7 us; the launch traced here: 76.5 us
  Pallas kernels  47.1 us (61%)
  waiting for transfers between devices  9.31 us (12%)
  matrix products  6.26 us (8%)
  local copies, waits for them, and re-layouts  5.16 us (7%)
  starting transfers between devices  4.17 us (5%)
  other arithmetic  3.67 us (5%)
  between operations  0.84 us (1%)
    pallas_call x1, Pallas kernels, reduce_all(): pl.pallas_call(reduce_kernel, out_shape=(jax.ShapeDtypeStruct((t_blk[0] /...  47.1 us
    ppermute x1, waiting for transfers between devices, on_small_slice(): lax.ppermute(give, 'tm', [(i, (i + shards // 2) % shards) for i in range(...  7.71 us
    unnamed x10, local copies, waits for them, and re-layouts  5.06 us
    ppermute x1, starting transfers between devices, on_small_slice(): lax.ppermute(give, 'tm', [(i, (i + shards // 2) % shards) for i in range(...  4.1 us
    dot_general x4, matrix products, project(): jnp.dot(rows, weight, preferred_element_type=jnp.float32)  2.45 us
    dot_general x3, matrix products, project_back(): lax.dot_general(rows, weight, (((1,), (1,)), ((), ())), preferred_element...  2.15 us
    transpose x1, other arithmetic, on_small_slice(): grad_out = o_sum.astype(F32).T  1.69 us
    convert_element_type x1, other arithmetic, on_small_slice(): grad_in = i_sum.astype(F32)  1.69 us
  transfers between devices with their start and end apart: 2, of which 2 were waited for; matrix products, arithmetic and copies ran while one was open for 0% of the time, Pallas kernels for 0%

profile of v5, /device:TPU:0, one launch (start us, length us, event | category | flops | bytes accessed | tf_op | source)
XLA Modules:
  0.0 76.5 jit_solution(11493186086522450073)
XLA Ops:
  0.6 1.2 %copy.13 = bf16[1,128,576]{2,1,0:T(8,128)(2,1)S(1)} copy(bf16[1,128,576]{1,2,0:T(8,128)(2,1)} %param.5) | data formatting | bytes 294912 | tf_op args[0]
  1.8 1.1 %copy.14 = bf16[1,128,576]{2,1,0:T(8,128)(2,1)S(1)} copy(bf16[1,128,576]{1,2,0:T(8,128)(2,1)} %param.9) | data formatting | bytes 294912 | tf_op args[4]
  2.9 4.1 %collective-permute-start = (bf16[2,64,576]{2,1,0:T(8,128)(2,1)S(1)}, bf16[2,64,576]{2,1,0:T(8,128)(2,1)S(1)}, u32[]{:S(2)}, u32[]{:S(2)}) collective-permute-start(bf16[2,64,576]{2,1,0:T(8,128)(2,1)S(1)} %broadcast_select_fusion), channel_id=1, source_target_pairs={{0,4},{1,5},{2,6},{3,7},{4,0},{5,1},{6,2},{7,3},{8,12},{9,13},{10,... | collective-permute-start | bytes 442376 | tf_op jit(solution)/shard_map/ppermute | solution.py:348
  7.0 7.7 %collective-permute-done = bf16[2,64,576]{2,1,0:T(8,128)(2,1)S(1)} collective-permute-done((bf16[2,64,576]{2,1,0:T(8,128)(2,1)S(1)}, bf16[2,64,576]{2,1,0:T(8,128)(2,1)S(1)}, u32[]{:S(2)}, u32[]{:S(2)}) %collective-permute-start) | collective-permute-done | bytes 147488 | tf_op jit(solution)/shard_map/ppermute | solution.py:348
  14.8 0.1 select_bitcast_fusion.1
  15.0 1.6 %collective-permute-done.1 = bf16[2,2,64,576]{3,2,1,0:T(8,128)(2,1)S(1)} collective-permute-done((bf16[2,2,64,576]{3,2,1,0:T(8,128)(2,1)S(1)}, bf16[2,2,64,576]{3,2,1,0:T(8,128)(2,1)S(1)}, u32[]{:S(2)}, u32[]{:S(2)}) %collective-permute-start.1) | collective-permute-done | bytes 294944 | tf_op jit(solution)/shard_map/ppermute | solution.py:351
  16.6 0.1 pad_maximum_fusion
  16.8 0.6 convolution_convert_fusion.4
  17.4 1.4 %copy-done.2 = bf16[1,2048,1024]{2,1,0:T(8,128)(2,1)S(1)} copy-done((bf16[1,2048,1024]{2,1,0:T(8,128)(2,1)S(1)}, bf16[1,2048,1024]{2,1,0:T(8,128)(2,1)}, u32[]{:S(2)}) %copy-start.2) | copy-done | bytes 4194328
  18.8 0.4 fusion.2
  19.3 0.6 fusion.52
  19.8 0.9 %add_convert_fusion = (bf16[256,1024]{1,0:T(8,128)(2,1)S(1)}, bf16[256,1024]{1,0:T(8,128)(2,1)S(1)}) fusion(bf16[256,1024]{1,0:T(8,128)(2,1)S(1)} %convolution_convert_fusion.4, f32[256,1024]{1,0:T(8,128)S(1)} %fusion.52, f32[128,1024]{1,0:T(8,128)S(1)} %fusion.2, bf16[1,2048,1024]{2,1,0:T(8,128)(2,1)S(1)} %copy-done.2), kind=kOutput, calls=%fused_computation.23 | convolution fusion | flops 538968064 | bytes 5767168 | tf_op jit(solution)/shard_map/dot_general | solution.py:20
  20.7 0.7 fusion.4
  21.5 0.8 %fusion = f32[128,1024]{1,0:T(8,128)S(1)} fusion(bf16[1,2048,1024]{2,1,0:T(8,128)(2,1)S(1)} %copy-done.2, bf16[256,1024]{1,0:T(8,128)(2,1)S(1)} %get-tuple-element.13), kind=kOutput, calls=%fused_computation.4 | convolution fusion | flops 268435456 | bytes 2883584 | tf_op jit(solution)/shard_map/dot_general | solution.py:27
  22.3 0.3 convolution_convert_fusion.2.o_ref
  22.7 0.5 convolution_convert_fusion.1
  23.2 0.5 convolution_convert_fusion
  23.7 0.5 fusion.29.p_ref
  24.2 0.4 convolution_convert_fusion.3.i_ref
  24.6 47.1 %shard_map.84 = (f32[64,1024]{1,0:T(8,128)S(1)}, bf16[576,1024]{1,0:T(8,128)(2,1)S(1)}, bf16[576,1024]{1,0:T(8,128)(2,1)S(1)}, f32[576,128]{1,0:T(8,128)S(1)}) custom-call(bf16[4,4,128,256]{3,2,1,0:T(8,128)(2,1)S(1)} %bitcast.42, bf16[4,4,128,256]{3,2,1,0:T(8,128)(2,1)S(1)} %bitcast.43, bf16[576,512]{1,0:T(8,128)(2,1)S(1)} %convolution_convert_fusion.3.i_ref, ...), custom_call_target="tpu_custom_call" | custom-call | tf_op jit(solution)/shard_map/pallas_call | solution.py:317
  71.7 1.7 %convert_bitcast_fusion = f32[1024,576]{0,1:T(8,128)} fusion(bf16[576,1024]{1,0:T(8,128)(2,1)S(1)} %get-tuple-element.11), kind=kLoop, calls=%fused_computation.2 | loop fusion | flops 589824 | bytes 3538944 | tf_op jit(solution)/shard_map/transpose | solution.py:389
  73.4 1.7 %convert_element_type.40 = f32[576,1024]{1,0:T(8,128)} convert(bf16[576,1024]{1,0:T(8,128)(2,1)S(1)} %get-tuple-element.9) | non-fusion elementwise | flops 589824 | bytes 3538944 | tf_op jit(solution)/shard_map/convert_element_type | solution.py:388
  75.1 0.7 copy.21
  75.8 0.7 copy.22
  (12 shorter events, 0.3 us)
Async XLA Ops:
  0.6 18.6 %copy-start = (bf16[1024,576]{0,1:T(8,128)(2,1)S(1)}, bf16[1024,576]{0,1:T(8,128)(2,1)}, u32[]{:S(2)}) copy-start(bf16[1024,576]{0,1:T(8,128)(2,1)} %param.8) | copy-start | bytes 3538948
  2.9 13.9 %copy-start.1 = (bf16[576,1024]{1,0:T(8,128)(2,1)S(1)}, bf16[576,1024]{1,0:T(8,128)(2,1)}, u32[]{:S(2)}) copy-start(bf16[576,1024]{1,0:T(8,128)(2,1)} %param.6) | copy-start | bytes 3538948
  2.9 11.8 %collective-permute-start = (bf16[2,64,576]{2,1,0:T(8,128)(2,1)S(1)}, bf16[2,64,576]{2,1,0:T(8,128)(2,1)S(1)}, u32[]{:S(2)}, u32[]{:S(2)}) collective-permute-start(bf16[2,64,576]{2,1,0:T(8,128)(2,1)S(1)} %broadcast_select_fusion), channel_id=1, source_target_pairs={{0,4},{1,5},{2,6},{3,7},{4,0},{5,1},{6,2},{7,3},{8,12},{9,13},{10,... | collective-permute-start | bytes 442376 | tf_op jit(solution)/shard_map/ppermute | solution.py:348
  14.9 1.7 %collective-permute-start.1 = (bf16[2,2,64,576]{3,2,1,0:T(8,128)(2,1)S(1)}, bf16[2,2,64,576]{3,2,1,0:T(8,128)(2,1)S(1)}, u32[]{:S(2)}, u32[]{:S(2)}) collective-permute-start(bf16[2,2,64,576]{3,2,1,0:T(8,128)(2,1)S(1)} %get-tuple-element.20), channel_id=1, source_target_pairs={{0,1},{1,0},{2,3},{3,2},{4,5},{5,4},{6,7},{7,6},{8,9},{9,8},{10,11... | collective-permute-start | bytes 884744 | tf_op jit(solution)/shard_map/ppermute | solution.py:351
  16.6 2.2 %copy-start.2 = (bf16[1,2048,1024]{2,1,0:T(8,128)(2,1)S(1)}, bf16[1,2048,1024]{2,1,0:T(8,128)(2,1)}, u32[]{:S(2)}) copy-start(bf16[1,2048,1024]{2,1,0:T(8,128)(2,1)} %param.7) | copy-start | bytes 12582916
